TPU v7x, 512 devices: a whole 4x4x16 slice. The times are simulated.
512 devices in a mesh: seq: 128 (over x, y, z_lo), head: 4 (over z_hi, core).
Axes of the slice: x: 4, y: 4, z: 16 (z_hi: 2, z_lo: 8; z = z_hi * 8 + z_lo), core: 2. Of those that a mesh axis runs over, the one named last changes fastest.
Arguments:
- queries: bfloat16 [65536, 4096], P('seq', 'head'), may hold values from -80 to 80
- keys_next: bfloat16 [65536, 1024], P('seq', 'head'), may hold values from -4 to 4
- values_next: bfloat16 [65536, 1024], P('seq', 'head'), may hold values from -6 to 6
- keys_front: bfloat16 [1024, 1024], P(None, 'head'), may hold values from -4 to 4
- values_front: bfloat16 [1024, 1024], P(None, 'head'), may hold values from -6 to 6
- keys_prev: bfloat16 [65536, 1024], P('seq', 'head'), may hold values from -6 to 6
- values_prev: bfloat16 [65536, 1024], P('seq', 'head'), may hold values from -6 to 6
Outputs:
- attended: bfloat16 [65536, 4096], P('seq', 'head')
- banded_keys: bfloat16 [65536, 1024], P('seq', 'head')
- banded_values: bfloat16 [65536, 1024], P('seq', 'head')
All inputs are finite; a program needn't handle non-finite values.
Results may differ from a plain program's by a relative error of at most 0.0075.
Values may be sent and summed in bfloat16 or wider, within the bound.
No kernel may reach another device: no remote copies, remote signals or barrier semaphores. Data moves between devices by JAX's collectives and lax.ppermute only.
A program may use at most 64 MiB of HBM per device.

v0:
```python
import jax
import jax.numpy as jnp
from jax import lax
from jax.sharding import PartitionSpec as P

QH = 32
KVH = 8
HD = 128


def shifted(value, axis, steps):
    count = lax.axis_size(axis)
    leading, last = (max(0, -steps), min(count, count - steps))
    return lax.ppermute(value, axis, [(source, source + steps) for source in range(leading, last)])


def sent_together(arrays, axis, split_dim, concat_dim, along):
    widths = [a.shape[along] for a in arrays]
    both = jnp.concatenate(arrays, axis=along)
    out = lax.all_to_all(both, axis, split_axis=split_dim, concat_axis=concat_dim, tiled=True)
    return tuple(jnp.split(out, [sum(widths[:k]) for k in range(1, len(widths))], axis=along))


def group_attention(query_rows, keys_window, values_window, visible):
    scores = jnp.einsum(
        "srd,td->rst", query_rows, keys_window, preferred_element_type=jnp.float32
    ) * HD ** (-0.5)
    masked = jnp.where(visible, scores, -jnp.inf)
    top = jnp.max(masked, axis=-1, keepdims=True)
    mass = jnp.where(visible, jnp.exp(masked - top), 0.0)
    total = jnp.sum(mass, axis=-1)
    weights = mass.astype(jnp.bfloat16)
    summed = jnp.einsum("rst,td->rsd", weights, values_window, preferred_element_type=jnp.float32)
    result = summed / total[..., None]
    return jnp.transpose(result, (1, 0, 2))


def shards(queries, keys_next, values_next, keys_front, values_front, keys_prev, values_prev):
    rows = queries.shape[0]
    width = keys_next.shape[1]
    groups = width // HD
    ratio = QH // KVH
    position = lax.axis_index("seq")
    own_block = jnp.concatenate([keys_next, values_next], axis=1)
    front_block = jnp.concatenate([keys_front, values_front], axis=1)
    front_early = front_block[:rows]
    front_late = front_block[rows:]
    received = shifted(own_block, "seq", 1)
    prior = jnp.where(position == 0, front_late, received)
    relayed = shifted(prior, "seq", 1)
    second = jnp.where(position == 0, front_early, relayed)
    window = jnp.concatenate([second, prior, own_block], axis=0)
    keys_window = window[:, :width]
    values_window = window[:, width:]
    query_idx = jnp.arange(rows, dtype=jnp.int32)
    key_idx = jnp.arange(3 * rows, dtype=jnp.int32)
    visible = key_idx[None, :] <= query_idx[:, None] + 2 * rows
    outputs = []
    for kv_group in range(groups):
        query_rows = queries[:, kv_group * ratio * HD : (kv_group + 1) * ratio * HD].reshape(
            rows, ratio, HD
        )
        keys_group = keys_window[:, kv_group * HD : (kv_group + 1) * HD]
        values_group = values_window[:, kv_group * HD : (kv_group + 1) * HD]
        piece = group_attention(query_rows, keys_group, values_group, visible)
        outputs.append(piece.reshape(rows, ratio * HD))
    attended = jnp.concatenate(outputs, axis=1).astype(jnp.bfloat16)
    devices = lax.axis_size("seq")
    lanes = rows // devices
    moved_keys, moved_values = sent_together(
        (keys_prev.reshape(lanes, devices, width), values_prev.reshape(lanes, devices, width)),
        "seq",
        1,
        0,
        2,
    )
    banded_keys = moved_keys.reshape(rows, width)
    banded_values = moved_values.reshape(rows, width)
    return (attended, banded_keys, banded_values)


def solution(mesh):
    in_specs = (
        P("seq", "head"),
        P("seq", "head"),
        P("seq", "head"),
        P(None, "head"),
        P(None, "head"),
        P("seq", "head"),
        P("seq", "head"),
    )
    out_specs = (P("seq", "head"), P("seq", "head"), P("seq", "head"))
    return jax.shard_map(shards, mesh=mesh, in_specs=in_specs, out_specs=out_specs, check_vma=False)
```

profile of v0, /device:TPU:414, one launch (start us, length us, event | category | flops | bytes accessed | tf_op | source)
XLA Modules:
  0.0 95.2 jit_solution(3161592699651390711)
XLA Ops:
  0.6 1.0 %constant_dynamic-update-slice_fusion.3 = bf16[512,512]{1,0:T(8,128)(2,1)S(1)} fusion(bf16[512,256]{1,0:T(8,128)(2,1)} %param.8), kind=kLoop, calls=%fused_computation.43 | loop fusion | bytes 524288
  1.6 1.0 %constant_dynamic-update-slice_fusion.2 = bf16[512,512]{1,0:T(8,128)(2,1)S(1)} fusion(bf16[512,512]{1,0:T(8,128)(2,1)S(1)} %constant_dynamic-update-slice_fusion.3, bf16[512,256]{1,0:T(8,128)(2,1)} %param.9), kind=kLoop, calls=%fused_computation.42 | loop fusion | bytes 524288 | tf_op jit(solution)/shard_map/concatenate | solution.py:44
  2.6 2.9 %collective-permute-start = (bf16[512,512]{1,0:T(8,128)(2,1)S(1)}, bf16[512,512]{1,0:T(8,128)(2,1)}, u32[]{:S(2)}, u32[]{:S(2)}) collective-permute-start(bf16[512,512]{1,0:T(8,128)(2,1)S(1)} %constant_dynamic-update-slice_fusion.2), channel_id=1, source_target_pairs={{0,4},{4,8},{8,12},{12,16},{16,20},{20,24},{24,28},{28,32},{32,36}... | collective-permute-start | bytes 1572872 | tf_op jit(solution)/shard_map/ppermute | solution.py:14
  5.5 1.2 %copy.28 = bf16[4,128,256]{2,0,1:T(4,128)(2,1)S(1)} copy(bf16[4,128,256]{2,1,0:T(8,128)(2,1)} %bitcast.92) | data formatting | bytes 524288 | tf_op jit(solution)/shard_map/reshape | solution.py:71
  6.7 1.2 %copy.29 = bf16[4,128,256]{2,0,1:T(4,128)(2,1)S(1)} copy(bf16[4,128,256]{2,1,0:T(8,128)(2,1)} %bitcast.93) | data formatting | bytes 524288 | tf_op jit(solution)/shard_map/reshape | solution.py:71
  7.8 1.0 %pad_maximum_fusion.2 = bf16[4,128,512]{2,0,1:T(4,128)(2,1)} fusion(bf16[4,128,256]{2,0,1:T(4,128)(2,1)S(1)} %copy.29, bf16[4,128,256]{2,0,1:T(4,128)(2,1)S(1)} %copy.28), kind=kLoop, calls=%fused_computation.31 | loop fusion | flops 1048576 | bytes 1048576 | tf_op jit(solution)/shard_map/concatenate | solution.py:19
  8.9 19.9 %all-to-all-start = ((bf16[4,128,512]{2,0,1:T(4,128)(2,1)}), bf16[4,128,512]{2,0,1:T(4,128)(2,1)S(1)}, u32[]{:S(2)}, u32[]{:S(2)}) async-start(bf16[4,128,512]{2,0,1:T(4,128)(2,1)} %pad_maximum_fusion.2), calls=%async_computation | async-start | bytes 1048576 | tf_op jit(solution)/shard_map/all_to_all | solution.py:20
  28.8 1.1 %constant_dynamic-update-slice_fusion.1 = bf16[1024,512]{1,0:T(8,128)(2,1)S(1)} fusion(bf16[1024,256]{1,0:T(8,128)(2,1)} %param.10), kind=kLoop, calls=%fused_computation.41 | loop fusion | bytes 1048576
  29.9 1.1 %constant_dynamic-update-slice_fusion = bf16[1024,512]{1,0:T(8,128)(2,1)S(1)} fusion(bf16[1024,512]{1,0:T(8,128)(2,1)S(1)} %constant_dynamic-update-slice_fusion.1, bf16[1024,256]{1,0:T(8,128)(2,1)} %param.11), kind=kLoop, calls=%fused_computation.40 | loop fusion | bytes 1048576 | tf_op jit(solution)/shard_map/concatenate | solution.py:45
  31.0 1.3 %fusion.42 = (bf16[512,512]{1,0:T(8,128)(2,1)S(1)}, bf16[512,512]{1,0:T(8,128)(2,1)S(1)}) fusion(bf16[512,1024]{1,0:T(8,128)(2,1)} %param.7), kind=kLoop, calls=%fused_computation.49 | loop fusion | bytes 2097152 | tf_op jit(solution)/shard_map/slice | solution.py:60
  32.3 1.1 %slice_select_fusion = bf16[512,512]{1,0:T(8,128)(2,1)S(1)} fusion(bf16[512,512]{1,0:T(8,128)(2,1)} %collective-permute-done, bf16[1024,512]{1,0:T(8,128)(2,1)S(1)} %constant_dynamic-update-slice_fusion, pred[]{:T(512)S(6)} %eq.4), kind=kLoop, calls=%fused_computation.29 | loop fusion | flops 262144 | bytes 1572865 | tf_op jit(solution)/shard_map/jit(_where)/select_n | solution.py:49
  33.4 3.6 %collective-permute-start.1 = (bf16[512,512]{1,0:T(8,128)(2,1)S(1)}, bf16[512,512]{1,0:T(8,128)(2,1)}, u32[]{:S(2)}, u32[]{:S(2)}) collective-permute-start(bf16[512,512]{1,0:T(8,128)(2,1)S(1)} %slice_select_fusion), channel_id=1, source_target_pairs={{0,4},{4,8},{8,12},{12,16},{16,20},{20,24},{24,28},{28,32},{32,36}... | collective-permute-start | bytes 1572872 | tf_op jit(solution)/shard_map/ppermute | solution.py:14
  36.9 1.0 %copy.38 = bf16[512,512]{0,1:T(8,128)(2,1)} copy(bf16[512,512]{1,0:T(8,128)(2,1)S(1)} %get-tuple-element.3) | data formatting | bytes 1048576
  38.0 1.0 %copy.39 = bf16[512,512]{0,1:T(8,128)(2,1)} copy(bf16[512,512]{1,0:T(8,128)(2,1)S(1)} %get-tuple-element.4) | data formatting | bytes 1048576
  39.6 22.7 %collective-permute-done.1 = bf16[512,512]{1,0:T(8,128)(2,1)} collective-permute-done((bf16[512,512]{1,0:T(8,128)(2,1)S(1)}, bf16[512,512]{1,0:T(8,128)(2,1)}, u32[]{:S(2)}, u32[]{:S(2)}) %collective-permute-start.1) | collective-permute-done | bytes 524320 | tf_op jit(solution)/shard_map/ppermute | solution.py:14
  62.3 1.1 %slice_select_fusion.1 = bf16[512,512]{1,0:T(8,128)(2,1)S(1)} fusion(bf16[512,512]{1,0:T(8,128)(2,1)} %collective-permute-done.1, bf16[1024,512]{1,0:T(8,128)(2,1)S(1)} %constant_dynamic-update-slice_fusion, pred[]{:T(512)S(6)} %eq.4), kind=kLoop, calls=%fused_computation.30 | loop fusion | flops 262144 | bytes 1572865 | tf_op jit(solution)/shard_map/jit(_where)/select_n | solution.py:51
  63.4 2.3 %pad_maximum_fusion = bf16[1536,512]{1,0:T(8,128)(2,1)} fusion(bf16[512,512]{1,0:T(8,128)(2,1)} %copy-done.1, bf16[512,512]{1,0:T(8,128)(2,1)S(1)} %slice_select_fusion, bf16[512,512]{1,0:T(8,128)(2,1)S(1)} %slice_select_fusion.1), kind=kLoop, calls=%fused_computation.19 | loop fusion | flops 4718592 | bytes 3145728 | tf_op jit(solution)/shard_map/concatenate | solution.py:52
  65.7 8.8 %fusion.44 = (f32[4,512]{1,0:T(4,128)S(1)}, bf16[4,512,1536]{1,2,0:T(8,128)(2,1)}) fusion(pred[512,1536]{0,1:T(8,128)(4,1)S(1)} %iota_compare_fusion, bf16[512,4,128]{0,2,1:T(8,128)(2,1)S(1)} %bitcast.89, bf16[1536,512]{1,0:T(8,128)(2,1)} %pad_maximum_fusion), kind=kOutput, calls=%fused_computation.51 | convolution fusion | flops 824182272 | bytes 8790016 | tf_op jit(solution)/shard_map/sub | solution.py:30
  74.5 4.6 %fusion.30 = bf16[512,4,128]{0,2,1:T(8,128)(2,1)} fusion(bf16[4,512,1536]{1,2,0:T(8,128)(2,1)} %get-tuple-element.10, f32[512,4]{0,1:T(4,128)S(1)} %bitcast.95, bf16[1536,512]{1,0:T(8,128)(2,1)S(1)} %copy-done), kind=kOutput, calls=%fused_computation.26 | convolution fusion | flops 805830656 | bytes 7217152 | tf_op jit(solution)/shard_map/rst,td->rsd/dot_general | solution.py:33
  79.1 1.3 %copy.26 = bf16[512,512]{1,0:T(8,128)(2,1)S(1)} copy(bf16[512,512]{0,1:T(8,128)(2,1)} %bitcast.91) | data formatting | bytes 1048576 | tf_op jit(solution)/shard_map/reshape | solution.py:66
  80.4 8.6 %fusion.43 = (f32[4,512]{1,0:T(4,128)S(1)}, bf16[4,512,1536]{1,2,0:T(8,128)(2,1)}) fusion(pred[512,1536]{0,1:T(8,128)(4,1)S(1)} %iota_compare_fusion, bf16[512,4,128]{0,2,1:T(8,128)(2,1)} %bitcast.88, bf16[1536,512]{1,0:T(8,128)(2,1)S(1)} %copy-done), kind=kOutput, calls=%fused_computation.50 | convolution fusion | flops 824182272 | bytes 8790016 | tf_op jit(solution)/shard_map/sub | solution.py:30
  89.0 3.8 %fusion.33 = bf16[512,4,128]{0,2,1:T(8,128)(2,1)S(1)} fusion(bf16[4,512,1536]{1,2,0:T(8,128)(2,1)} %get-tuple-element.8, f32[512,4]{0,1:T(4,128)S(1)} %bitcast.94, bf16[1536,512]{1,0:T(8,128)(2,1)S(1)} %copy-done), kind=kOutput, calls=%fused_computation.27 | convolution fusion | flops 805830656 | bytes 7217152 | tf_op jit(solution)/shard_map/rst,td->rsd/dot_general | solution.py:33
  93.1 1.1 %pad_maximum_fusion.1 = bf16[512,1024]{1,0:T(8,128)(2,1)} fusion(bf16[512,512]{1,0:T(8,128)(2,1)S(1)} %copy.27, bf16[512,512]{1,0:T(8,128)(2,1)S(1)} %copy.26), kind=kLoop, calls=%fused_computation.28 | loop fusion | flops 2097152 | bytes 2097152 | tf_op jit(solution)/shard_map/concatenate | solution.py:67
  94.3 0.8 slice_bitcast_fusion.18
  (12 shorter events, 1.0 us)
Async XLA Ops:
  2.6 29.7 %copy-start.1 = (bf16[512,512]{1,0:T(8,128)(2,1)}, bf16[512,512]{1,0:T(8,128)(2,1)S(1)}, u32[]{:S(2)}) copy-start(bf16[512,512]{1,0:T(8,128)(2,1)S(1)} %constant_dynamic-update-slice_fusion.2) | copy-start | bytes 1572868
  2.6 29.7 %collective-permute-start = (bf16[512,512]{1,0:T(8,128)(2,1)S(1)}, bf16[512,512]{1,0:T(8,128)(2,1)}, u32[]{:S(2)}, u32[]{:S(2)}) collective-permute-start(bf16[512,512]{1,0:T(8,128)(2,1)S(1)} %constant_dynamic-update-slice_fusion.2), channel_id=1, source_target_pairs={{0,4},{4,8},{8,12},{12,16},{16,20},{20,24},{24,28},{28,32},{32,36}... | collective-permute-start | bytes 1572872 | tf_op jit(solution)/shard_map/ppermute | solution.py:14
  8.9 85.3 %all-to-all-start = ((bf16[4,128,512]{2,0,1:T(4,128)(2,1)}), bf16[4,128,512]{2,0,1:T(4,128)(2,1)S(1)}, u32[]{:S(2)}, u32[]{:S(2)}) async-start(bf16[4,128,512]{2,0,1:T(4,128)(2,1)} %pad_maximum_fusion.2), calls=%async_computation | async-start | bytes 1048576 | tf_op jit(solution)/shard_map/all_to_all | solution.py:20
  33.4 28.9 %collective-permute-start.1 = (bf16[512,512]{1,0:T(8,128)(2,1)S(1)}, bf16[512,512]{1,0:T(8,128)(2,1)}, u32[]{:S(2)}, u32[]{:S(2)}) collective-permute-start(bf16[512,512]{1,0:T(8,128)(2,1)S(1)} %slice_select_fusion), channel_id=1, source_target_pairs={{0,4},{4,8},{8,12},{12,16},{16,20},{20,24},{24,28},{28,32},{32,36}... | collective-permute-start | bytes 1572872 | tf_op jit(solution)/shard_map/ppermute | solution.py:14
  38.0 27.7 %copy-start.2 = (bf16[512,512]{0,1:T(8,128)(2,1)S(1)}, bf16[512,512]{0,1:T(8,128)(2,1)}, u32[]{:S(2)}) copy-start(bf16[512,512]{0,1:T(8,128)(2,1)} %copy.38) | copy-start | bytes 1572868
  65.7 8.8 %copy-start = (bf16[1536,512]{1,0:T(8,128)(2,1)S(1)}, bf16[1536,512]{1,0:T(8,128)(2,1)}, u32[]{:S(2)}) copy-start(bf16[1536,512]{1,0:T(8,128)(2,1)} %pad_maximum_fusion) | copy-start | bytes 4718596
where the time goes:
time: 96.1 us; the launch traced here: 95.2 us
  starting transfers between devices  26.4 us (27%)
  matrix products  25.9 us (27%)
  waiting for transfers between devices  22.7 us (24%)
  local copies, waits for them, and re-layouts  12.1 us (13%)
  other arithmetic  7.27 us (8%)
    ppermute x2, waiting for transfers between devices, shifted(): lax.ppermute(value, axis, [(source, source + steps) for source in range(l...  22.7 us
    all_to_all x1, starting transfers between devices, sent_together(): lax.all_to_all(both, axis, split_axis=split_dim, concat_axis=concat_dim,...  19.9 us
    sub x2, matrix products, group_attention(): mass = jnp.where(visible, jnp.exp(masked - top), 0.0)  17.4 us
    dot_general x2, matrix products, group_attention(): jnp.einsum('rst,td->rsd', weights, values_window, preferred_element_type=...  8.46 us
    ppermute x2, starting transfers between devices, shifted(): lax.ppermute(value, axis, [(source, source + steps) for source in range(l...  6.49 us
    unnamed x10, local copies, waits for them, and re-layouts  4.08 us
    concatenate x1, other arithmetic, shards(): window = jnp.concatenate([second, prior, own_block], axis=0)  2.29 us
  transfers between devices with their start and end apart: 3, of which 1 were waited for; matrix products, arithmetic and copies ran while one was open for 45% of the time, Pallas kernels for 0%

commit v1 on v0

v1 whole, which is shorter than its diff:
```python
import functools

import jax
import jax.numpy as jnp
from jax import lax
from jax.experimental import pallas as pl
from jax.experimental.pallas import tpu as pltpu
from jax.sharding import PartitionSpec as P


QH = 32
KVH = 8
HD = 128
RATIO = QH // KVH
ROWS = 512
WIDTH = 256
HEADS = 8
NZ = 8
NXY = 16
EXP_SCALE = 1.4426950408889634 * HD**-0.5
HALF = 256

XY_GROUPS = [[z + NZ * c for c in range(NXY)] for z in range(NZ)]
Z_GROUPS = [[NZ * c + z for z in range(NZ)] for c in range(NXY)]


def shifted(value):
    count = lax.axis_size("seq")
    return lax.ppermute(value, "seq", [(source, source + 1) for source in range(count - 1)])


def vmem():
    return pl.BlockSpec(memory_space=pltpu.VMEM)


def anywhere():
    return pl.BlockSpec(memory_space=pl.ANY)


def smem():
    return pl.BlockSpec(memory_space=pltpu.SMEM)


def cost(flops, moved):
    return pl.CostEstimate(flops=flops, bytes_accessed=moved, transcendentals=0)


def pack_kernel(keys_ref, values_ref, out_ref, sems):
    copies = []
    for kv, ref in enumerate((keys_ref, values_ref)):
        for k in range(4):
            copies.append(
                pltpu.make_async_copy(
                    ref.at[k], out_ref.at[:, pl.ds(kv * 32 + k * 8, 8), :], sems.at[kv * 4 + k]
                )
            )
    for copy in copies:
        copy.start()
    for copy in copies:
        copy.wait()


def pack(keys, values):
    return pl.pallas_call(
        pack_kernel,
        out_shape=jax.ShapeDtypeStruct((NXY, 64, WIDTH), jnp.bfloat16),
        in_specs=[anywhere(), anywhere()],
        out_specs=vmem(),
        scratch_shapes=[pltpu.SemaphoreType.DMA((8,))],
        cost_estimate=cost(0, 1 << 20),
        name="pack",
    )(keys.reshape(4, NXY, 8, WIDTH), values.reshape(4, NXY, 8, WIDTH))


def chooser(source_of_row):
    row = lax.broadcasted_iota(jnp.int32, (128, 128), 0)
    col = lax.broadcasted_iota(jnp.int32, (128, 128), 1)
    return jnp.where(col == source_of_row(row), 1.0, 0.0).astype(jnp.bfloat16)


def middle_kernel(x_ref, out_ref):
    pick = chooser(lambda r: (r & 15) * 8 + (r >> 4))
    for kv in range(2):
        for c in range(4):
            rows = jnp.concatenate(
                [x_ref[c * 4 + s, pl.ds(kv * 32, 32), :] for s in range(4)], axis=0
            )
            moved = jnp.dot(pick, rows, preferred_element_type=jnp.float32).astype(jnp.bfloat16)
            for z in range(NZ):
                out_ref[z, pl.ds(kv * 64 + c * 16, 16), :] = moved[z * 16 : (z + 1) * 16, :]


def middle(x):
    return pl.pallas_call(
        middle_kernel,
        out_shape=jax.ShapeDtypeStruct((NZ, 128, WIDTH), jnp.bfloat16),
        in_specs=[vmem()],
        out_specs=vmem(),
        cost_estimate=cost(1 << 26, 1 << 20),
        name="middle",
    )(x)


def final_kernel(x_ref, keys_ref, values_ref):
    pick = chooser(lambda r: ((r >> 2) & 7) * 16 + (r >> 5) * 4 + (r & 3))
    for kv, ref in enumerate((keys_ref, values_ref)):
        for c in range(4):
            rows = jnp.concatenate(
                [x_ref[z, pl.ds(kv * 64 + c * 16, 16), :] for z in range(NZ)], axis=0
            )
            moved = jnp.dot(pick, rows, preferred_element_type=jnp.float32)
            ref[pl.ds(c * 128, 128), :] = moved.astype(jnp.bfloat16)


def final(x):
    shape = jax.ShapeDtypeStruct((ROWS, WIDTH), jnp.bfloat16)
    return pl.pallas_call(
        final_kernel,
        out_shape=(shape, shape),
        in_specs=[vmem()],
        out_specs=(vmem(), vmem()),
        cost_estimate=cost(1 << 26, 1 << 20),
        name="final",
    )(x)


def scores_of(q, keys):
    return lax.dot_general(
        q, keys, (((1,), (1,)), ((), ())), preferred_element_type=jnp.float32
    )


def fetch(choices, keys_buf, values_buf, sems):
    for when, keys_src, values_src in choices:

        @pl.when(when)
        def _(keys_src=keys_src, values_src=values_src):
            keys_copy = pltpu.make_async_copy(keys_src, keys_buf, sems.at[0])
            values_copy = pltpu.make_async_copy(values_src, values_buf, sems.at[1])
            keys_copy.start()
            values_copy.start()
            keys_copy.wait()
            values_copy.wait()


def head_slices(h):
    mine = pl.ds(pl.multiple_of(h * HD, HD), HD)
    group = pl.ds(pl.multiple_of((h // RATIO) * HD, HD), HD)
    return mine, group


def near_kernel(
    pos_ref, q_ref, k0_ref, v0_ref, k1_ref, v1_ref, kf_ref, vf_ref,
    o_ref, m_ref, l_ref, k_buf, v_buf, sems,
):
    pos = pos_ref[0]
    late = pl.ds(ROWS, ROWS)
    fetch(
        ((pos == 0, kf_ref.at[late], vf_ref.at[late]), (pos != 0, k1_ref, v1_ref)),
        k_buf, v_buf, sems,
    )
    lane = lax.broadcasted_iota(jnp.int32, (HALF, 128), 1)
    row = lax.broadcasted_iota(jnp.int32, (HALF, HALF), 0)
    col = lax.broadcasted_iota(jnp.int32, (HALF, HALF), 1)
    visible = col <= row

    def body(h, carry):
        mine, group = head_slices(h)
        for i in range(ROWS // HALF):
            span = pl.ds(i * HALF, HALF)
            q = q_ref[span, mine]
            parts = [(scores_of(q, k_buf[:, group]), v_buf[:, group])]
            if i > 0:
                before = pl.ds(0, i * HALF)
                parts.append((scores_of(q, k0_ref[before, group]), v0_ref[before, group]))
            own = scores_of(q, k0_ref[span, group])
            parts.append((jnp.where(visible, own, -jnp.inf), v0_ref[span, group]))
            top = functools.reduce(
                jnp.maximum, [jnp.max(s, axis=1, keepdims=True) for s, _ in parts]
            )
            total = jnp.zeros((HALF, 1), jnp.float32)
            summed = jnp.zeros((HALF, HD), jnp.float32)
            for s, values in parts:
                mass = jnp.exp2((s - top) * EXP_SCALE)
                total += jnp.sum(mass, axis=1, keepdims=True)
                summed += jnp.dot(
                    mass.astype(jnp.bfloat16), values, preferred_element_type=jnp.float32
                )
            o_ref[span, mine] = summed
            m_ref[span, :] = jnp.where(lane == h, top, m_ref[span, :])
            l_ref[span, :] = jnp.where(lane == h, total, l_ref[span, :])
        return carry

    m_ref[...] = jnp.zeros_like(m_ref)
    l_ref[...] = jnp.zeros_like(l_ref)
    lax.fori_loop(0, HEADS, body, 0)


def near(pos, q, k0, v0, k1, v1, kf, vf):
    stat = jax.ShapeDtypeStruct((ROWS, 128), jnp.float32)
    return pl.pallas_call(
        near_kernel,
        out_shape=(jax.ShapeDtypeStruct((ROWS, HEADS * HD), jnp.float32), stat, stat),
        in_specs=[smem(), vmem(), vmem(), vmem(), anywhere(), anywhere(), anywhere(), anywhere()],
        out_specs=(vmem(), vmem(), vmem()),
        scratch_shapes=[
            pltpu.VMEM((ROWS, WIDTH), jnp.bfloat16),
            pltpu.VMEM((ROWS, WIDTH), jnp.bfloat16),
            pltpu.SemaphoreType.DMA((2,)),
        ],
        cost_estimate=cost(3 << 30, 5 << 20),
        name="near",
    )(pos, q, k0, v0, k1, v1, kf, vf)


def far_kernel(
    pos_ref, q_ref, k2_ref, v2_ref, kf_ref, vf_ref, o_ref, m_ref, l_ref,
    out_ref, k_buf, v_buf, sems,
):
    pos = pos_ref[0]
    early = pl.ds(0, ROWS)
    late = pl.ds(ROWS, ROWS)
    fetch(
        (
            (pos == 0, kf_ref.at[early], vf_ref.at[early]),
            (pos == 1, kf_ref.at[late], vf_ref.at[late]),
            (pos > 1, k2_ref, v2_ref),
        ),
        k_buf, v_buf, sems,
    )
    lane = lax.broadcasted_iota(jnp.int32, (HALF, 128), 1)

    def body(h, carry):
        mine, group = head_slices(h)
        for i in range(ROWS // HALF):
            span = pl.ds(i * HALF, HALF)
            s = scores_of(q_ref[span, mine], k_buf[:, group])
            old_top = jnp.sum(jnp.where(lane == h, m_ref[span, :], 0.0), axis=1, keepdims=True)
            old_total = jnp.sum(jnp.where(lane == h, l_ref[span, :], 0.0), axis=1, keepdims=True)
            top = jnp.maximum(jnp.max(s, axis=1, keepdims=True), old_top)
            mass = jnp.exp2((s - top) * EXP_SCALE)
            keep = jnp.exp2((old_top - top) * EXP_SCALE)
            total = keep * old_total + jnp.sum(mass, axis=1, keepdims=True)
            summed = keep * o_ref[span, mine] + jnp.dot(
                mass.astype(jnp.bfloat16), v_buf[:, group], preferred_element_type=jnp.float32
            )
            out_ref[span, mine] = (summed / total).astype(jnp.bfloat16)
        return carry

    lax.fori_loop(0, HEADS, body, 0)


def far(pos, q, k2, v2, kf, vf, o, m, l):
    return pl.pallas_call(
        far_kernel,
        out_shape=jax.ShapeDtypeStruct((ROWS, HEADS * HD), jnp.bfloat16),
        in_specs=[smem(), vmem(), anywhere(), anywhere(), anywhere(), anywhere(), vmem(), vmem(), vmem()],
        out_specs=vmem(),
        scratch_shapes=[
            pltpu.VMEM((ROWS, WIDTH), jnp.bfloat16),
            pltpu.VMEM((ROWS, WIDTH), jnp.bfloat16),
            pltpu.SemaphoreType.DMA((2,)),
        ],
        cost_estimate=cost(2 << 30, 5 << 20),
        name="far",
    )(pos, q, k2, v2, kf, vf, o, m, l)


def exchange(x, groups):
    return lax.all_to_all(
        x, "seq", split_axis=0, concat_axis=0, tiled=True, axis_index_groups=groups
    )


def shards(queries, keys_next, values_next, keys_front, values_front, keys_prev, values_prev):
    pos = lax.axis_index("seq").astype(jnp.int32).reshape(1)
    k1 = shifted(keys_next)
    v1 = shifted(values_next)
    k2 = shifted(k1)
    v2 = shifted(v1)
    packed = pack(keys_prev, values_prev)
    crossed = exchange(packed, XY_GROUPS)
    mixed = middle(crossed)
    arrived = exchange(mixed, Z_GROUPS)
    state = near(pos, queries, keys_next, values_next, k1, v1, keys_front, values_front)
    attended = far(pos, queries, k2, v2, keys_front, values_front, *state)
    banded_keys, banded_values = final(arrived)
    return (attended, banded_keys, banded_values)


def solution(mesh):
    in_specs = (
        P("seq", "head"),
        P("seq", "head"),
        P("seq", "head"),
        P(None, "head"),
        P(None, "head"),
        P("seq", "head"),
        P("seq", "head"),
    )
    out_specs = (P("seq", "head"), P("seq", "head"), P("seq", "head"))
    return jax.shard_map(
        shards, mesh=mesh, in_specs=in_specs, out_specs=out_specs, check_vma=False
    )
```

time: 96.1 us -> 100 us (1.041)
  the two profiles are of different devices: /device:TPU:414 before, /device:TPU:96 now
where the time goes in v1:
time: 100 us; the launch traced here: 99.6 us
  starting transfers between devices  30.7 us (31%)
  Pallas kernels  28.9 us (29%)
  waiting for transfers between devices  19 us (19%)
  blocking collectives  18.6 us (19%)
  local copies, waits for them, and re-layouts  1.57 us (2%)
    ppermute x4, waiting for transfers between devices, shifted(): lax.ppermute(value, 'seq', [(source, source + 1) for source in range(coun...  19 us
    ppermute x4, starting transfers between devices, shifted(): lax.ppermute(value, 'seq', [(source, source + 1) for source in range(coun...  18.9 us
    all_to_all x1, blocking collectives, exchange(): lax.all_to_all(x, 'seq', split_axis=0, concat_axis=0, tiled=True, axis_in...  18.6 us
    pallas_call x1, Pallas kernels, near(): pl.pallas_call(near_kernel, out_shape=(jax.ShapeDtypeStruct((ROWS, HEADS...  12.6 us
    all_to_all x1, starting transfers between devices, exchange(): lax.all_to_all(x, 'seq', split_axis=0, concat_axis=0, tiled=True, axis_in...  11.7 us
    pallas_call x1, Pallas kernels, far(): pl.pallas_call(far_kernel, out_shape=jax.ShapeDtypeStruct((ROWS, HEADS *...  10.2 us
    pallas_call x1, Pallas kernels, middle(): pl.pallas_call(middle_kernel, out_shape=jax.ShapeDtypeStruct((NZ, 128, WI...  2.12 us
    pallas_call x1, Pallas kernels, final(): pl.pallas_call(final_kernel, out_shape=(shape, shape), in_specs=[vmem()],...  2.04 us
  transfers between devices with their start and end apart: 5, of which 1 were waited for; matrix products, arithmetic and copies ran while one was open for 0% of the time, Pallas kernels for 23%

profile of v1, /device:TPU:96, one launch (start us, length us, event | category | flops | bytes accessed | tf_op | source)
XLA Modules:
  0.0 99.6 jit_solution(13004715524113557105)
XLA Ops:
  0.6 0.0 copy-start.1
  0.6 0.0 copy-start.2
  0.7 2.0 %pack.1 = bf16[16,64,256]{2,1,0:T(8,128)(2,1)} custom-call(bf16[4,16,8,256]{3,2,1,0:T(8,128)(2,1)} %bitcast.3, bf16[4,16,8,256]{3,2,1,0:T(8,128)(2,1)} %bitcast.4), custom_call_target="tpu_custom_call" | custom-call | bytes 1048576 | tf_op jit(solution)/shard_map/pack/pallas_call | solution.py:64
  2.6 18.6 %all_to_all.10.x_ref = bf16[16,64,256]{2,1,0:T(8,128)(2,1)} all-to-all(bf16[16,64,256]{2,1,0:T(8,128)(2,1)} %pack.1), channel_id=1, replica_groups={{0,32,64,96,128,160,192,224,256,288,320,352,384,416,448,480},{4,36,68,1..., dimensions={0} | all-to-all | bytes 1048576 | tf_op jit(solution)/shard_map/all_to_all | solution.py:270
  21.3 2.1 %middle.1 = bf16[8,128,256]{2,1,0:T(8,128)(2,1)} custom-call(bf16[16,64,256]{2,1,0:T(8,128)(2,1)} %all_to_all.10.x_ref), custom_call_target="tpu_custom_call" | custom-call | flops 67108864 | bytes 1048576 | tf_op jit(solution)/shard_map/middle/pallas_call | solution.py:94
  23.4 11.7 %all-to-all-start.1 = ((bf16[8,128,256]{2,1,0:T(8,128)(2,1)}), bf16[8,128,256]{2,1,0:T(8,128)(2,1)S(1)}, u32[]{:S(2)}, u32[]{:S(2)}) async-start(bf16[8,128,256]{2,1,0:T(8,128)(2,1)} %middle.1), calls=%async_computation.1 | async-start | bytes 1048576 | tf_op jit(solution)/shard_map/all_to_all | solution.py:270
  35.1 4.6 %collective-permute-start = (bf16[512,256]{1,0:T(8,128)(2,1)S(1)}, bf16[512,256]{1,0:T(8,128)(2,1)S(1)}, u32[]{:S(2)}, u32[]{:S(2)}) collective-permute-start(bf16[512,256]{1,0:T(8,128)(2,1)S(1)} %copy-done.1), channel_id=1, source_target_pairs={{0,4},{4,8},{8,12},{12,16},{16,20},{20,24},{24,28},{28,32},{32,36}... | collective-permute-start | bytes 786440 | tf_op jit(solution)/shard_map/ppermute | solution.py:29
  39.7 3.4 %collective-permute-start.2 = (bf16[512,256]{1,0:T(8,128)(2,1)S(1)}, bf16[512,256]{1,0:T(8,128)(2,1)S(1)}, u32[]{:S(2)}, u32[]{:S(2)}) collective-permute-start(bf16[512,256]{1,0:T(8,128)(2,1)S(1)} %copy-done.2), channel_id=1, source_target_pairs={{0,4},{4,8},{8,12},{12,16},{16,20},{20,24},{24,28},{28,32},{32,36}... | collective-permute-start | bytes 786440 | tf_op jit(solution)/shard_map/ppermute | solution.py:29
  43.1 19.0 %collective-permute-done.k1_ref = bf16[512,256]{1,0:T(8,128)(2,1)S(1)} collective-permute-done((bf16[512,256]{1,0:T(8,128)(2,1)S(1)}, bf16[512,256]{1,0:T(8,128)(2,1)S(1)}, u32[]{:S(2)}, u32[]{:S(2)}) %collective-permute-start) | collective-permute-done | bytes 262176 | tf_op jit(solution)/shard_map/ppermute | solution.py:29
  62.1 5.6 %collective-permute-start.1 = (bf16[512,256]{1,0:T(8,128)(2,1)S(1)}, bf16[512,256]{1,0:T(8,128)(2,1)S(1)}, u32[]{:S(2)}, u32[]{:S(2)}) collective-permute-start(bf16[512,256]{1,0:T(8,128)(2,1)S(1)} %collective-permute-done.k1_ref), channel_id=1, source_target_pairs={{0,4},{4,8},{8,12},{12,16},{16,20},{20,24},{24,28},{28,32},{32,36}... | collective-permute-start | bytes 786440 | tf_op jit(solution)/shard_map/ppermute | solution.py:29
  67.7 0.0 collective-permute-done.2.v1_ref
  67.7 0.0 copy-start.4
  67.7 5.4 %collective-permute-start.3 = (bf16[512,256]{1,0:T(8,128)(2,1)S(1)}, bf16[512,256]{1,0:T(8,128)(2,1)S(1)}, u32[]{:S(2)}, u32[]{:S(2)}) collective-permute-start(bf16[512,256]{1,0:T(8,128)(2,1)S(1)} %collective-permute-done.2.v1_ref), channel_id=1, source_target_pairs={{0,4},{4,8},{8,12},{12,16},{16,20},{20,24},{24,28},{28,32},{32,36}... | collective-permute-start | bytes 786440 | tf_op jit(solution)/shard_map/ppermute | solution.py:29
  73.2 12.6 %near.1 = (f32[512,1024]{1,0:T(8,128)}, f32[512,128]{1,0:T(8,128)}, f32[512,128]{1,0:T(8,128)}) custom-call(s32[1]{0:T(128)} %bitcast.pos_ref, bf16[512,1024]{1,0:T(8,128)(2,1)} %q_ref.3, bf16[512,256]{1,0:T(8,128)(2,1)} %k0_ref.1, bf16[512,256]{1,0:T(8,128)(2,1)} %v0_ref.1, bf16[512,256]{1,0:T(8,128)(2,1)} %copy-done.3, bf16[512,256]{1,0:T(8,128)(2,1)} %copy-done.4, ...), custom_call_target="tpu_custom_call" | custom-call | flops 3221225472 | bytes 5242880 | tf_op jit(solution)/shard_map/near/pallas_call | solution.py:201
  85.8 0.0 collective-permute-done.1.k2_ref
  85.8 0.0 copy-start.5
  85.8 0.0 collective-permute-done.3.v2_ref
  85.8 0.0 copy-start.6
  85.8 0.7 copy-done.5
  86.5 0.1 copy-done.6
  86.6 10.2 %far.1 = bf16[512,1024]{1,0:T(8,128)(2,1)} custom-call(s32[1]{0:T(128)} %bitcast.pos_ref, bf16[512,1024]{1,0:T(8,128)(2,1)} %q_ref.3, bf16[512,256]{1,0:T(8,128)(2,1)} %copy-done.5, bf16[512,256]{1,0:T(8,128)(2,1)} %copy-done.6, bf16[1024,256]{1,0:T(8,128)(2,1)} %kf_ref.3, bf16[1024,256]{1,0:T(8,128)(2,1)} %vf_ref.3, f32[512,1024]{1,0:T(8,128)} %get-tuple-element.8.o_ref, ...), custom_call_target="tpu_custom_call" | custom-call | flops 2147483648 | bytes 5242880 | tf_op jit(solution)/shard_map/far/pallas_call | solution.py:254
  96.8 0.0 all-to-all-done.1.x_ref
  96.8 0.8 copy-done
  97.6 2.0 %final.1 = (bf16[512,256]{1,0:T(8,128)(2,1)}, bf16[512,256]{1,0:T(8,128)(2,1)}) custom-call(bf16[8,128,256]{2,1,0:T(8,128)(2,1)} %copy-done), custom_call_target="tpu_custom_call" | custom-call | flops 67108864 | bytes 1048576 | tf_op jit(solution)/shard_map/final/pallas_call | solution.py:117
  (6 shorter events, 0.0 us)
Async XLA Ops:
  0.6 34.5 %copy-start.1 = (bf16[512,256]{1,0:T(8,128)(2,1)S(1)}, bf16[512,256]{1,0:T(8,128)(2,1)}, u32[]{:S(2)}) copy-start(bf16[512,256]{1,0:T(8,128)(2,1)} %k0_ref.1) | copy-start | bytes 786436
  0.6 39.1 %copy-start.2 = (bf16[512,256]{1,0:T(8,128)(2,1)S(1)}, bf16[512,256]{1,0:T(8,128)(2,1)}, u32[]{:S(2)}) copy-start(bf16[512,256]{1,0:T(8,128)(2,1)} %v0_ref.1) | copy-start | bytes 786436
  23.4 73.4 %all-to-all-start.1 = ((bf16[8,128,256]{2,1,0:T(8,128)(2,1)}), bf16[8,128,256]{2,1,0:T(8,128)(2,1)S(1)}, u32[]{:S(2)}, u32[]{:S(2)}) async-start(bf16[8,128,256]{2,1,0:T(8,128)(2,1)} %middle.1), calls=%async_computation.1 | async-start | bytes 1048576 | tf_op jit(solution)/shard_map/all_to_all | solution.py:270
  35.1 27.0 %collective-permute-start = (bf16[512,256]{1,0:T(8,128)(2,1)S(1)}, bf16[512,256]{1,0:T(8,128)(2,1)S(1)}, u32[]{:S(2)}, u32[]{:S(2)}) collective-permute-start(bf16[512,256]{1,0:T(8,128)(2,1)S(1)} %copy-done.1), channel_id=1, source_target_pairs={{0,4},{4,8},{8,12},{12,16},{16,20},{20,24},{24,28},{28,32},{32,36}... | collective-permute-start | bytes 786440 | tf_op jit(solution)/shard_map/ppermute | solution.py:29
  39.7 28.0 %collective-permute-start.2 = (bf16[512,256]{1,0:T(8,128)(2,1)S(1)}, bf16[512,256]{1,0:T(8,128)(2,1)S(1)}, u32[]{:S(2)}, u32[]{:S(2)}) collective-permute-start(bf16[512,256]{1,0:T(8,128)(2,1)S(1)} %copy-done.2), channel_id=1, source_target_pairs={{0,4},{4,8},{8,12},{12,16},{16,20},{20,24},{24,28},{28,32},{32,36}... | collective-permute-start | bytes 786440 | tf_op jit(solution)/shard_map/ppermute | solution.py:29
  62.1 11.0 %copy-start.3 = (bf16[512,256]{1,0:T(8,128)(2,1)}, bf16[512,256]{1,0:T(8,128)(2,1)S(1)}, u32[]{:S(2)}) copy-start(bf16[512,256]{1,0:T(8,128)(2,1)S(1)} %collective-permute-done.k1_ref) | copy-start | bytes 786436
  62.1 23.6 %collective-permute-start.1 = (bf16[512,256]{1,0:T(8,128)(2,1)S(1)}, bf16[512,256]{1,0:T(8,128)(2,1)S(1)}, u32[]{:S(2)}, u32[]{:S(2)}) collective-permute-start(bf16[512,256]{1,0:T(8,128)(2,1)S(1)} %collective-permute-done.k1_ref), channel_id=1, source_target_pairs={{0,4},{4,8},{8,12},{12,16},{16,20},{20,24},{24,28},{28,32},{32,36}... | collective-permute-start | bytes 786440 | tf_op jit(solution)/shard_map/ppermute | solution.py:29
  67.7 5.4 %copy-start.4 = (bf16[512,256]{1,0:T(8,128)(2,1)}, bf16[512,256]{1,0:T(8,128)(2,1)S(1)}, u32[]{:S(2)}) copy-start(bf16[512,256]{1,0:T(8,128)(2,1)S(1)} %collective-permute-done.2.v1_ref) | copy-start | bytes 786436
  67.7 18.0 %collective-permute-start.3 = (bf16[512,256]{1,0:T(8,128)(2,1)S(1)}, bf16[512,256]{1,0:T(8,128)(2,1)S(1)}, u32[]{:S(2)}, u32[]{:S(2)}) collective-permute-start(bf16[512,256]{1,0:T(8,128)(2,1)S(1)} %collective-permute-done.2.v1_ref), channel_id=1, source_target_pairs={{0,4},{4,8},{8,12},{12,16},{16,20},{20,24},{24,28},{28,32},{32,36}... | collective-permute-start | bytes 786440 | tf_op jit(solution)/shard_map/ppermute | solution.py:29
  85.8 0.7 copy-start.5
  85.8 0.8 copy-start.6
  96.8 0.8 copy-start

commit v2 on v1

v2 whole, which is shorter than its diff:
```python
import functools

import jax
import jax.numpy as jnp
from jax import lax
from jax.experimental import pallas as pl
from jax.experimental.pallas import tpu as pltpu
from jax.sharding import PartitionSpec as P


QH = 32
KVH = 8
HD = 128
RATIO = QH // KVH
ROWS = 512
WIDTH = 256
HEADS = 8
EXP_SCALE = 1.4426950408889634 * HD**-0.5
NEAR = 256
FAR = 256
LIMIT = 24 << 20


def shifted(value):
    count = lax.axis_size("seq")
    return lax.ppermute(value, "seq", [(source, source + 1) for source in range(count - 1)])


def vmem():
    return pl.BlockSpec(memory_space=pltpu.VMEM)


def anywhere():
    return pl.BlockSpec(memory_space=pl.ANY)


def smem():
    return pl.BlockSpec(memory_space=pltpu.SMEM)


def cost(flops, moved):
    return pl.CostEstimate(flops=flops, bytes_accessed=moved, transcendentals=0)


def chooser(size, source_of_row):
    row = lax.broadcasted_iota(jnp.int32, (size, size), 0)
    col = lax.broadcasted_iota(jnp.int32, (size, size), 1)
    return jnp.where(col == source_of_row(row), 1.0, 0.0).astype(jnp.bfloat16)


def moved_by(pick, parts):
    rows = jnp.concatenate(parts, axis=0) if len(parts) > 1 else parts[0]
    return jnp.dot(pick, rows, preferred_element_type=jnp.float32).astype(jnp.bfloat16)


def pack_kernel(k_ref, v_ref, out_ref):
    pick = chooser(128, lambda r: (r & 7) * 16 + (r >> 3))
    for c in range(8):
        out_ref[pl.ds(c * 128, 128), :] = moved_by(
            pick, [ref[pl.ds(k * 128 + c * 16, 16), :] for ref in (k_ref, v_ref) for k in range(4)])


def pack(keys, values):
    packed = pl.pallas_call(
        pack_kernel,
        out_shape=jax.ShapeDtypeStruct((2 * ROWS, WIDTH), jnp.bfloat16),
        in_specs=[vmem(), vmem()],
        out_specs=vmem(),
        cost_estimate=cost(1 << 26, 1 << 20),
        name="pack",
    )(keys, values)
    return packed.reshape(ROWS // 4, 8, WIDTH)


def unpack_kernel(x_ref, k_ref, v_ref):
    pick = chooser(128, lambda r: ((r >> 2) & 15) * 8 + (r >> 6) * 4 + (r & 3))
    for c in range(8):
        moved = moved_by(pick, [x_ref[pl.ds(c * 128, 128), :]])
        k_ref[pl.ds(c * 64, 64), :] = moved[:64]
        v_ref[pl.ds(c * 64, 64), :] = moved[64:]


def unpack(x):
    shape = jax.ShapeDtypeStruct((ROWS, WIDTH), jnp.bfloat16)
    return pl.pallas_call(
        unpack_kernel,
        out_shape=(shape, shape),
        in_specs=[vmem()],
        out_specs=(vmem(), vmem()),
        compiler_params=pltpu.CompilerParams(vmem_limit_bytes=8 << 20),
        cost_estimate=cost(1 << 26, 1 << 20),
        name="unpack",
    )(x.reshape(2 * ROWS, WIDTH))


def exchange(x):
    return lax.all_to_all(
        x, "seq", split_axis=0, concat_axis=0, tiled=True
    )


def scores_of(q, keys):
    return lax.dot_general(
        q, keys, (((1,), (1,)), ((), ())), preferred_element_type=jnp.float32
    )


def fetch(choices, keys_buf, wide_buf, sems):
    for when, keys_src, values_src in choices:

        @pl.when(when)
        def _(keys_src=keys_src, values_src=values_src):
            copies = [pltpu.make_async_copy(keys_src, keys_buf, sems.at[0])]
            for g in range(2):
                copies.append(
                    pltpu.make_async_copy(
                        values_src.at[:, pl.ds(g * HD, HD)],
                        wide_buf.at[g, :, pl.ds(0, HD)],
                        sems.at[1 + g],
                    )
                )
            for copy in copies:
                copy.start()
            for copy in copies:
                copy.wait()


def set_ones(wide_buf):
    for g in range(2):
        wide_buf[g, :, HD:] = jnp.ones_like(wide_buf[g, :, HD:])


def near_kernel(
    pos_ref, q_ref, k0_ref, v0_ref, k1_ref, v1_ref, kf_ref, vf_ref,
    o_ref, m_ref, l_ref, k_buf, wide1, wide0, sems,
):
    pos = pos_ref[0]
    late = pl.ds(ROWS, ROWS)
    fetch(
        ((pos == 0, kf_ref.at[late], vf_ref.at[late]), (pos != 0, k1_ref, v1_ref)),
        k_buf, wide1, sems,
    )
    set_ones(wide1)
    set_ones(wide0)
    for g in range(2):
        wide0[g, :, :HD] = v0_ref[:, g * HD : (g + 1) * HD]
    row = lax.broadcasted_iota(jnp.int32, (NEAR, NEAR), 0)
    col = lax.broadcasted_iota(jnp.int32, (NEAR, NEAR), 1)
    visible = col <= row
    for h in range(HEADS):
        g = h // RATIO
        mine = slice(h * HD, (h + 1) * HD)
        group = slice(g * HD, (g + 1) * HD)
        for i in range(ROWS // NEAR):
            lo, hi = i * NEAR, (i + 1) * NEAR
            q = q_ref[lo:hi, mine]
            parts = [(scores_of(q, k_buf[:, group]), wide1[g])]
            if i > 0:
                parts.append((scores_of(q, k0_ref[:lo, group]), wide0[g, :lo]))
            own = scores_of(q, k0_ref[lo:hi, group])
            parts.append((jnp.where(visible, own, -jnp.inf), wide0[g, lo:hi]))
            top = functools.reduce(
                jnp.maximum, [jnp.max(s, axis=1, keepdims=True) for s, _ in parts]
            )
            summed = jnp.zeros((NEAR, 2 * HD), jnp.float32)
            for s, values in parts:
                mass = jnp.exp2((s - top) * EXP_SCALE).astype(jnp.bfloat16)
                summed += jnp.dot(mass, values, preferred_element_type=jnp.float32)
            o_ref[lo:hi, mine] = summed[:, :HD]
            m_ref[lo:hi, h : h + 1] = top
            l_ref[lo:hi, h : h + 1] = summed[:, HD : HD + 1]


def block_scratch():
    return pltpu.VMEM((2, ROWS, 2 * HD), jnp.bfloat16)


def near(pos, q, k0, v0, k1, v1, kf, vf):
    stat = jax.ShapeDtypeStruct((ROWS, 128), jnp.float32)
    return pl.pallas_call(
        near_kernel,
        out_shape=(jax.ShapeDtypeStruct((ROWS, HEADS * HD), jnp.float32), stat, stat),
        in_specs=[smem(), vmem(), vmem(), vmem(), anywhere(), anywhere(), anywhere(), anywhere()],
        out_specs=(vmem(), vmem(), vmem()),
        scratch_shapes=[
            pltpu.VMEM((ROWS, WIDTH), jnp.bfloat16),
            block_scratch(),
            block_scratch(),
            pltpu.SemaphoreType.DMA((3,)),
        ],
        compiler_params=pltpu.CompilerParams(vmem_limit_bytes=LIMIT),
        cost_estimate=cost(3 << 30, 5 << 20),
        name="near",
    )(pos, q, k0, v0, k1, v1, kf, vf)


def far_kernel(
    pos_ref, q_ref, k2_ref, v2_ref, kf_ref, vf_ref, o_ref, m_ref, l_ref,
    out_ref, k_buf, wide, sems,
):
    pos = pos_ref[0]
    early = pl.ds(0, ROWS)
    late = pl.ds(ROWS, ROWS)
    set_ones(wide)
    fetch(
        (
            (pos == 0, kf_ref.at[early], vf_ref.at[early]),
            (pos == 1, kf_ref.at[late], vf_ref.at[late]),
            (pos > 1, k2_ref, v2_ref),
        ),
        k_buf, wide, sems,
    )
    for h in range(HEADS):
        g = h // RATIO
        mine = slice(h * HD, (h + 1) * HD)
        group = slice(g * HD, (g + 1) * HD)
        for i in range(ROWS // FAR):
            lo, hi = i * FAR, (i + 1) * FAR
            s = scores_of(q_ref[lo:hi, mine], k_buf[:, group])
            old_top = m_ref[lo:hi, h : h + 1]
            top = jnp.maximum(jnp.max(s, axis=1, keepdims=True), old_top)
            keep = jnp.exp2((old_top - top) * EXP_SCALE)
            mass = jnp.exp2((s - top) * EXP_SCALE).astype(jnp.bfloat16)
            summed = jnp.dot(mass, wide[g], preferred_element_type=jnp.float32)
            total = keep * l_ref[lo:hi, h : h + 1] + summed[:, HD:]
            out = (keep * o_ref[lo:hi, mine] + summed[:, :HD]) / total
            out_ref[lo:hi, mine] = out.astype(jnp.bfloat16)


def far(pos, q, k2, v2, kf, vf, o, m, l):
    return pl.pallas_call(
        far_kernel,
        out_shape=jax.ShapeDtypeStruct((ROWS, HEADS * HD), jnp.bfloat16),
        in_specs=[smem(), vmem(), anywhere(), anywhere(), anywhere(), anywhere(), vmem(), vmem(), vmem()],
        out_specs=vmem(),
        scratch_shapes=[
            pltpu.VMEM((ROWS, WIDTH), jnp.bfloat16),
            block_scratch(),
            pltpu.SemaphoreType.DMA((3,)),
        ],
        compiler_params=pltpu.CompilerParams(vmem_limit_bytes=LIMIT),
        cost_estimate=cost(2 << 30, 5 << 20),
        name="far",
    )(pos, q, k2, v2, kf, vf, o, m, l)


def shards(queries, keys_next, values_next, keys_front, values_front, keys_prev, values_prev):
    pos = lax.axis_index("seq").astype(jnp.int32).reshape(1)
    k1 = shifted(keys_next)
    v1 = shifted(values_next)
    k2 = shifted(k1)
    v2 = shifted(v1)
    packed = pack(keys_prev, values_prev)
    arrived = exchange(packed)
    state = near(pos, queries, keys_next, values_next, k1, v1, keys_front, values_front)
    attended = far(pos, queries, k2, v2, keys_front, values_front, *state)
    banded_keys, banded_values = unpack(arrived)
    return (attended, banded_keys, banded_values)


def solution(mesh):
    in_specs = (
        P("seq", "head"),
        P("seq", "head"),
        P("seq", "head"),
        P(None, "head"),
        P(None, "head"),
        P("seq", "head"),
        P("seq", "head"),
    )
    out_specs = (P("seq", "head"), P("seq", "head"), P("seq", "head"))
    return jax.shard_map(
        shards, mesh=mesh, in_specs=in_specs, out_specs=out_specs, check_vma=False
    )
```

time: 100 us -> 80.8 us (0.81)
  the two profiles are of different devices: /device:TPU:96 before, /device:TPU:6 now
where the time goes in v2:
time: 80.8 us; the launch traced here: 80.5 us
  waiting for transfers between devices  32.2 us (40%)
  starting transfers between devices  30.5 us (38%)
  Pallas kernels  15.1 us (19%)
  local copies, waits for them, and re-layouts  1.91 us (2%)
    ppermute x4, waiting for transfers between devices, shifted(): lax.ppermute(value, 'seq', [(source, source + 1) for source in range(coun...  32.2 us
    all_to_all x1, starting transfers between devices, exchange(): return lax.all_to_all(x, 'seq', split_axis=0, concat_axis=0, tiled=True)  20 us
    ppermute x4, starting transfers between devices, shifted(): lax.ppermute(value, 'seq', [(source, source + 1) for source in range(coun...  10.6 us
    pallas_call x1, Pallas kernels, near(): pl.pallas_call(near_kernel, out_shape=(jax.ShapeDtypeStruct((ROWS, HEADS...  5.95 us
    pallas_call x1, Pallas kernels, far(): pl.pallas_call(far_kernel, out_shape=jax.ShapeDtypeStruct((ROWS, HEADS *...  5.8 us
    pallas_call x1, Pallas kernels, pack(): pl.pallas_call(pack_kernel, out_shape=jax.ShapeDtypeStruct((2 * ROWS, WID...  2.26 us
    unnamed x10, local copies, waits for them, and re-layouts  1.91 us
  transfers between devices with their start and end apart: 5, of which 4 were waited for; matrix products, arithmetic and copies ran while one was open for 0% of the time, Pallas kernels for 15%

profile of v2, /device:TPU:6, one launch (start us, length us, event | category | flops | bytes accessed | tf_op | source)
XLA Modules:
  0.0 80.5 jit_solution(11796310883371347806)
XLA Ops:
  0.6 0.0 copy-start.1
  0.6 0.0 copy-start.2
  0.7 0.0 copy-start
  0.7 2.3 %pack.1 = bf16[1024,256]{1,0:T(8,128)(2,1)} custom-call(bf16[512,256]{1,0:T(8,128)(2,1)} %k_ref.1, bf16[512,256]{1,0:T(8,128)(2,1)} %v_ref.1), custom_call_target="tpu_custom_call" | custom-call | flops 67108864 | bytes 1048576 | tf_op jit(solution)/shard_map/pack/pallas_call | solution.py:64
  2.9 20.0 %all-to-all-start = ((bf16[128,8,256]{2,1,0:T(8,128)(2,1)}), bf16[128,8,256]{2,1,0:T(8,128)(2,1)S(1)}, u32[]{:S(2)}, u32[]{:S(2)}) async-start(bf16[128,8,256]{2,1,0:T(8,128)(2,1)} %bitcast.4), calls=%async_computation | async-start | bytes 1048576 | tf_op jit(solution)/shard_map/all_to_all | solution.py:97
  22.9 3.4 %collective-permute-start = (bf16[512,256]{1,0:T(8,128)(2,1)}, bf16[512,256]{1,0:T(8,128)(2,1)S(1)}, u32[]{:S(2)}, u32[]{:S(2)}) collective-permute-start(bf16[512,256]{1,0:T(8,128)(2,1)} %k0_ref.1), channel_id=1, source_target_pairs={{0,4},{4,8},{8,12},{12,16},{16,20},{20,24},{24,28},{28,32},{32,36}... | collective-permute-start | bytes 786440 | tf_op jit(solution)/shard_map/ppermute | solution.py:26
  26.3 3.4 %collective-permute-start.2 = (bf16[512,256]{1,0:T(8,128)(2,1)}, bf16[512,256]{1,0:T(8,128)(2,1)S(1)}, u32[]{:S(2)}, u32[]{:S(2)}) collective-permute-start(bf16[512,256]{1,0:T(8,128)(2,1)} %v0_ref.1), channel_id=1, source_target_pairs={{0,4},{4,8},{8,12},{12,16},{16,20},{20,24},{24,28},{28,32},{32,36}... | collective-permute-start | bytes 786440 | tf_op jit(solution)/shard_map/ppermute | solution.py:26
  29.7 20.1 %collective-permute-done.k1_ref = bf16[512,256]{1,0:T(8,128)(2,1)S(1)} collective-permute-done((bf16[512,256]{1,0:T(8,128)(2,1)}, bf16[512,256]{1,0:T(8,128)(2,1)S(1)}, u32[]{:S(2)}, u32[]{:S(2)}) %collective-permute-start) | collective-permute-done | bytes 262176 | tf_op jit(solution)/shard_map/ppermute | solution.py:26
  49.8 1.9 %collective-permute-start.1 = (bf16[512,256]{1,0:T(8,128)(2,1)S(1)}, bf16[512,256]{1,0:T(8,128)(2,1)S(1)}, u32[]{:S(2)}, u32[]{:S(2)}) collective-permute-start(bf16[512,256]{1,0:T(8,128)(2,1)S(1)} %collective-permute-done.k1_ref), channel_id=1, source_target_pairs={{0,4},{4,8},{8,12},{12,16},{16,20},{20,24},{24,28},{28,32},{32,36}... | collective-permute-start | bytes 786440 | tf_op jit(solution)/shard_map/ppermute | solution.py:26
  51.8 2.3 %collective-permute-done.2.v1_ref = bf16[512,256]{1,0:T(8,128)(2,1)S(1)} collective-permute-done((bf16[512,256]{1,0:T(8,128)(2,1)}, bf16[512,256]{1,0:T(8,128)(2,1)S(1)}, u32[]{:S(2)}, u32[]{:S(2)}) %collective-permute-start.2) | collective-permute-done | bytes 262176 | tf_op jit(solution)/shard_map/ppermute | solution.py:26
  54.0 1.9 %collective-permute-start.3 = (bf16[512,256]{1,0:T(8,128)(2,1)S(1)}, bf16[512,256]{1,0:T(8,128)(2,1)S(1)}, u32[]{:S(2)}, u32[]{:S(2)}) collective-permute-start(bf16[512,256]{1,0:T(8,128)(2,1)S(1)} %collective-permute-done.2.v1_ref), channel_id=1, source_target_pairs={{0,4},{4,8},{8,12},{12,16},{16,20},{20,24},{24,28},{28,32},{32,36}... | collective-permute-start | bytes 786440 | tf_op jit(solution)/shard_map/ppermute | solution.py:26
  56.0 0.0 copy-done.1
  56.0 0.0 copy-done.2
  56.0 0.0 copy-done
  56.0 0.0 copy-start.3
  56.0 0.9 %copy-done.3 = bf16[512,256]{1,0:T(8,128)(2,1)S(1)} copy-done((bf16[512,256]{1,0:T(8,128)(2,1)S(1)}, bf16[512,256]{1,0:T(8,128)(2,1)}, u32[]{:S(2)}) %copy-start.3) | copy-done | bytes 262168
  56.9 0.0 copy-start.4
  56.9 0.9 %copy-done.4 = bf16[512,256]{1,0:T(8,128)(2,1)S(1)} copy-done((bf16[512,256]{1,0:T(8,128)(2,1)S(1)}, bf16[512,256]{1,0:T(8,128)(2,1)}, u32[]{:S(2)}) %copy-start.4) | copy-done | bytes 262168
  57.9 6.0 %near.1 = (f32[512,1024]{1,0:T(8,128)S(1)}, f32[512,128]{1,0:T(8,128)S(1)}, f32[512,128]{1,0:T(8,128)S(1)}) custom-call(s32[1]{0:T(128)} %bitcast.pos_ref, bf16[512,1024]{1,0:T(8,128)(2,1)S(1)} %copy-done, bf16[512,256]{1,0:T(8,128)(2,1)S(1)} %copy-done.3, bf16[512,256]{1,0:T(8,128)(2,1)S(1)} %copy-done.4, bf16[512,256]{1,0:T(8,128)(2,1)S(1)} %collective-permute-done.k1_ref, ...), custom_call_target="tpu_custom_call" | custom-call | flops 3221225472 | bytes 5242880 | tf_op jit(solution)/shard_map/near/pallas_call | solution.py:180
  63.9 5.0 %collective-permute-done.1.k2_ref = bf16[512,256]{1,0:T(8,128)(2,1)S(1)} collective-permute-done((bf16[512,256]{1,0:T(8,128)(2,1)S(1)}, bf16[512,256]{1,0:T(8,128)(2,1)S(1)}, u32[]{:S(2)}, u32[]{:S(2)}) %collective-permute-start.1) | collective-permute-done | bytes 262176 | tf_op jit(solution)/shard_map/ppermute | solution.py:26
  68.8 4.8 %collective-permute-done.3.v2_ref = bf16[512,256]{1,0:T(8,128)(2,1)S(1)} collective-permute-done((bf16[512,256]{1,0:T(8,128)(2,1)S(1)}, bf16[512,256]{1,0:T(8,128)(2,1)S(1)}, u32[]{:S(2)}, u32[]{:S(2)}) %collective-permute-start.3) | collective-permute-done | bytes 262176 | tf_op jit(solution)/shard_map/ppermute | solution.py:26
  73.6 5.8 %far.1 = bf16[512,1024]{1,0:T(8,128)(2,1)} custom-call(s32[1]{0:T(128)} %bitcast.pos_ref, bf16[512,1024]{1,0:T(8,128)(2,1)S(1)} %copy-done, bf16[512,256]{1,0:T(8,128)(2,1)S(1)} %collective-permute-done.1.k2_ref, bf16[512,256]{1,0:T(8,128)(2,1)S(1)} %collective-permute-done.3.v2_ref, bf16[1024,256]{1,0:T(8,128)(2,1)S(1)} %copy-done.1, ...), custom_call_target="tpu_custom_call" | custom-call | flops 2147483648 | bytes 5242880 | tf_op jit(solution)/shard_map/far/pallas_call | solution.py:231
  79.4 0.0 all-to-all-done
  79.4 1.1 %unpack.1 = (bf16[512,256]{1,0:T(8,128)(2,1)}, bf16[512,256]{1,0:T(8,128)(2,1)}) custom-call(bf16[1024,256]{1,0:T(8,128)(2,1)S(1)} %bitcast.3), custom_call_target="tpu_custom_call" | custom-call | flops 67108864 | bytes 1048576 | tf_op jit(solution)/shard_map/unpack/pallas_call | solution.py:85
Async XLA Ops:
  0.6 55.3 %copy-start.1 = (bf16[1024,256]{1,0:T(8,128)(2,1)S(1)}, bf16[1024,256]{1,0:T(8,128)(2,1)}, u32[]{:S(2)}) copy-start(bf16[1024,256]{1,0:T(8,128)(2,1)} %kf_ref.3) | copy-start | bytes 1572868
  0.6 55.3 %copy-start.2 = (bf16[1024,256]{1,0:T(8,128)(2,1)S(1)}, bf16[1024,256]{1,0:T(8,128)(2,1)}, u32[]{:S(2)}) copy-start(bf16[1024,256]{1,0:T(8,128)(2,1)} %vf_ref.3) | copy-start | bytes 1572868
  0.7 55.3 %copy-start = (bf16[512,1024]{1,0:T(8,128)(2,1)S(1)}, bf16[512,1024]{1,0:T(8,128)(2,1)}, u32[]{:S(2)}) copy-start(bf16[512,1024]{1,0:T(8,128)(2,1)} %q_ref.3) | copy-start | bytes 3145732
  2.9 76.5 %all-to-all-start = ((bf16[128,8,256]{2,1,0:T(8,128)(2,1)}), bf16[128,8,256]{2,1,0:T(8,128)(2,1)S(1)}, u32[]{:S(2)}, u32[]{:S(2)}) async-start(bf16[128,8,256]{2,1,0:T(8,128)(2,1)} %bitcast.4), calls=%async_computation | async-start | bytes 1048576 | tf_op jit(solution)/shard_map/all_to_all | solution.py:97
  22.9 26.9 %collective-permute-start = (bf16[512,256]{1,0:T(8,128)(2,1)}, bf16[512,256]{1,0:T(8,128)(2,1)S(1)}, u32[]{:S(2)}, u32[]{:S(2)}) collective-permute-start(bf16[512,256]{1,0:T(8,128)(2,1)} %k0_ref.1), channel_id=1, source_target_pairs={{0,4},{4,8},{8,12},{12,16},{16,20},{20,24},{24,28},{28,32},{32,36}... | collective-permute-start | bytes 786440 | tf_op jit(solution)/shard_map/ppermute | solution.py:26
  26.3 27.7 %collective-permute-start.2 = (bf16[512,256]{1,0:T(8,128)(2,1)}, bf16[512,256]{1,0:T(8,128)(2,1)S(1)}, u32[]{:S(2)}, u32[]{:S(2)}) collective-permute-start(bf16[512,256]{1,0:T(8,128)(2,1)} %v0_ref.1), channel_id=1, source_target_pairs={{0,4},{4,8},{8,12},{12,16},{16,20},{20,24},{24,28},{28,32},{32,36}... | collective-permute-start | bytes 786440 | tf_op jit(solution)/shard_map/ppermute | solution.py:26
  49.8 19.0 %collective-permute-start.1 = (bf16[512,256]{1,0:T(8,128)(2,1)S(1)}, bf16[512,256]{1,0:T(8,128)(2,1)S(1)}, u32[]{:S(2)}, u32[]{:S(2)}) collective-permute-start(bf16[512,256]{1,0:T(8,128)(2,1)S(1)} %collective-permute-done.k1_ref), channel_id=1, source_target_pairs={{0,4},{4,8},{8,12},{12,16},{16,20},{20,24},{24,28},{28,32},{32,36}... | collective-permute-start | bytes 786440 | tf_op jit(solution)/shard_map/ppermute | solution.py:26
  54.0 19.5 %collective-permute-start.3 = (bf16[512,256]{1,0:T(8,128)(2,1)S(1)}, bf16[512,256]{1,0:T(8,128)(2,1)S(1)}, u32[]{:S(2)}, u32[]{:S(2)}) collective-permute-start(bf16[512,256]{1,0:T(8,128)(2,1)S(1)} %collective-permute-done.2.v1_ref), channel_id=1, source_target_pairs={{0,4},{4,8},{8,12},{12,16},{16,20},{20,24},{24,28},{28,32},{32,36}... | collective-permute-start | bytes 786440 | tf_op jit(solution)/shard_map/ppermute | solution.py:26
  56.0 1.0 %copy-start.3 = (bf16[512,256]{1,0:T(8,128)(2,1)S(1)}, bf16[512,256]{1,0:T(8,128)(2,1)}, u32[]{:S(2)}) copy-start(bf16[512,256]{1,0:T(8,128)(2,1)} %k0_ref.1) | copy-start | bytes 786436
  56.9 0.9 %copy-start.4 = (bf16[512,256]{1,0:T(8,128)(2,1)S(1)}, bf16[512,256]{1,0:T(8,128)(2,1)}, u32[]{:S(2)}) copy-start(bf16[512,256]{1,0:T(8,128)(2,1)} %v0_ref.1) | copy-start | bytes 786436

commit v3 on v2

v3 whole, which is shorter than its diff:
```python
import jax
import jax.numpy as jnp
from jax import lax
from jax.experimental import pallas as pl
from jax.experimental.pallas import tpu as pltpu
from jax.sharding import PartitionSpec as P


QH = 32
KVH = 8
HD = 128
RATIO = QH // KVH
ROWS = 512
WIDTH = 256
HEADS = 8
RUN = 8
EXP_SCALE = 1.4426950408889634 * HD**-0.5
NEAR = 256
FAR = 256
LIMIT = 24 << 20


def shifted(value):
    count = lax.axis_size("seq")
    return lax.ppermute(value, "seq", [(source, source + 1) for source in range(count - 1)])


def crossing(value):
    count = lax.axis_size("seq")
    pairs = [(source, source + 2) for source in range(RUN - 2, count - 2, RUN)]
    return lax.ppermute(value, "seq", pairs)


def inner(value):
    count = lax.axis_size("seq")
    pairs = [(source, source + 1) for source in range(count) if source % RUN != RUN - 1]
    return lax.ppermute(value, "seq", pairs)


def vmem():
    return pl.BlockSpec(memory_space=pltpu.VMEM)


def anywhere():
    return pl.BlockSpec(memory_space=pl.ANY)


def smem():
    return pl.BlockSpec(memory_space=pltpu.SMEM)


def cost(flops, moved):
    return pl.CostEstimate(flops=flops, bytes_accessed=moved, transcendentals=0)


def chooser(size, source_of_row):
    row = lax.broadcasted_iota(jnp.int32, (size, size), 0)
    col = lax.broadcasted_iota(jnp.int32, (size, size), 1)
    return jnp.where(col == source_of_row(row), 1.0, 0.0).astype(jnp.bfloat16)


def moved_by(pick, parts):
    rows = jnp.concatenate(parts, axis=0) if len(parts) > 1 else parts[0]
    return jnp.dot(pick, rows, preferred_element_type=jnp.float32).astype(jnp.bfloat16)


def pack_kernel(k_ref, v_ref, out_ref):
    pick = chooser(128, lambda r: (r & 7) * 16 + (r >> 3))
    for c in range(8):
        out_ref[pl.ds(c * 128, 128), :] = moved_by(
            pick, [ref[pl.ds(k * 128 + c * 16, 16), :] for ref in (k_ref, v_ref) for k in range(4)])


def pack(keys, values):
    packed = pl.pallas_call(
        pack_kernel,
        out_shape=jax.ShapeDtypeStruct((2 * ROWS, WIDTH), jnp.bfloat16),
        in_specs=[vmem(), vmem()],
        out_specs=vmem(),
        cost_estimate=cost(1 << 26, 1 << 20),
        name="pack",
    )(keys, values)
    return packed.reshape(ROWS // 4, 8, WIDTH)


def unpack_kernel(x_ref, k_ref, v_ref):
    pick = chooser(128, lambda r: ((r >> 2) & 15) * 8 + (r >> 6) * 4 + (r & 3))
    for c in range(8):
        moved = moved_by(pick, [x_ref[pl.ds(c * 128, 128), :]])
        k_ref[pl.ds(c * 64, 64), :] = moved[:64]
        v_ref[pl.ds(c * 64, 64), :] = moved[64:]


def unpack(x):
    shape = jax.ShapeDtypeStruct((ROWS, WIDTH), jnp.bfloat16)
    return pl.pallas_call(
        unpack_kernel,
        out_shape=(shape, shape),
        in_specs=[vmem()],
        out_specs=(vmem(), vmem()),
        compiler_params=pltpu.CompilerParams(vmem_limit_bytes=8 << 20),
        cost_estimate=cost(1 << 26, 1 << 20),
        name="unpack",
    )(x.reshape(2 * ROWS, WIDTH))


def exchange(x):
    return lax.all_to_all(
        x, "seq", split_axis=0, concat_axis=0, tiled=True
    )


def scores_of(q, keys):
    return lax.dot_general(
        q, keys, (((1,), (1,)), ((), ())), preferred_element_type=jnp.float32
    )


def fetch(choices, sems):
    for when, moves in choices:

        @pl.when(when)
        def _(moves=moves):
            copies = [
                pltpu.make_async_copy(source, target, sems.at[n])
                for n, (source, target) in enumerate(moves)
            ]
            for copy in copies:
                copy.start()
            for copy in copies:
                copy.wait()


def set_ones(wide_buf):
    for g in range(2):
        wide_buf[g, :, HD:] = jnp.ones_like(wide_buf[g, :, HD:])


def widened(values_src, wide_buf):
    return [
        (values_src.at[:, pl.ds(g * HD, HD)], wide_buf.at[g, :, pl.ds(0, HD)]) for g in range(2)
    ]


def second_choices(pos, front, crossed, relayed):
    starts_run = lax.rem(pos, RUN) == 0
    return (
        (pos == 0, front.at[pl.ds(0, ROWS)]),
        (pos == 1, front.at[pl.ds(ROWS, ROWS)]),
        ((pos > 1) & starts_run, crossed),
        ((pos > 1) & jnp.logical_not(starts_run), relayed),
    )


def main_kernel(
    pos_ref, q_ref, k0_ref, v0_ref, k1_ref, v1_ref, k2_ref, kx_ref, kf_ref, vf_ref,
    o_ref, l_ref, p_ref, k1_buf, k2_buf, wide1, wide0, sems,
):
    pos = pos_ref[0]
    late = pl.ds(ROWS, ROWS)
    fetch(
        [
            (when, [(source, k2_buf)])
            for when, source in second_choices(pos, kf_ref, kx_ref, k2_ref)
        ],
        sems,
    )
    fetch(
        [
            (pos == 0, [(kf_ref.at[late], k1_buf)] + widened(vf_ref.at[late], wide1)),
            (pos != 0, [(k1_ref, k1_buf)] + widened(v1_ref, wide1)),
        ],
        sems,
    )
    set_ones(wide1)
    set_ones(wide0)
    for g in range(2):
        wide0[g, :, :HD] = v0_ref[:, g * HD : (g + 1) * HD]
    row = lax.broadcasted_iota(jnp.int32, (NEAR, NEAR), 0)
    col = lax.broadcasted_iota(jnp.int32, (NEAR, NEAR), 1)
    visible = col <= row
    for h in range(HEADS):
        g = h // RATIO
        mine = slice(h * HD, (h + 1) * HD)
        group = slice(g * HD, (g + 1) * HD)
        for i in range(ROWS // NEAR):
            lo, hi = i * NEAR, (i + 1) * NEAR
            q = q_ref[lo:hi, mine]
            second = scores_of(q, k2_buf[:, group])
            parts = [(scores_of(q, k1_buf[:, group]), wide1[g])]
            if i > 0:
                parts.append((scores_of(q, k0_ref[:lo, group]), wide0[g, :lo]))
            own = scores_of(q, k0_ref[lo:hi, group])
            parts.append((jnp.where(visible, own, -jnp.inf), wide0[g, lo:hi]))
            top = jnp.max(second, axis=1, keepdims=True)
            for s, _ in parts:
                top = jnp.maximum(top, jnp.max(s, axis=1, keepdims=True))
            p_ref[h, lo:hi, :] = jnp.exp2((second - top) * EXP_SCALE).astype(jnp.bfloat16)
            summed = jnp.zeros((NEAR, 2 * HD), jnp.float32)
            for s, values in parts:
                mass = jnp.exp2((s - top) * EXP_SCALE).astype(jnp.bfloat16)
                summed += jnp.dot(mass, values, preferred_element_type=jnp.float32)
            o_ref[lo:hi, mine] = summed[:, :HD]
            l_ref[lo:hi, h : h + 1] = summed[:, HD : HD + 1]


def block_scratch():
    return pltpu.VMEM((2, ROWS, 2 * HD), jnp.bfloat16)


def main(pos, q, k0, v0, k1, v1, k2, kx, kf, vf):
    return pl.pallas_call(
        main_kernel,
        out_shape=(
            jax.ShapeDtypeStruct((ROWS, HEADS * HD), jnp.float32),
            jax.ShapeDtypeStruct((ROWS, 128), jnp.float32),
            jax.ShapeDtypeStruct((HEADS, ROWS, ROWS), jnp.bfloat16),
        ),
        in_specs=[smem()] + [vmem()] * 3 + [anywhere()] * 6,
        out_specs=(vmem(), vmem(), vmem()),
        scratch_shapes=[
            pltpu.VMEM((ROWS, WIDTH), jnp.bfloat16),
            pltpu.VMEM((ROWS, WIDTH), jnp.bfloat16),
            block_scratch(),
            block_scratch(),
            pltpu.SemaphoreType.DMA((3,)),
        ],
        compiler_params=pltpu.CompilerParams(vmem_limit_bytes=LIMIT),
        cost_estimate=cost(5 << 30, 10 << 20),
        name="main",
    )(pos, q, k0, v0, k1, v1, k2, kx, kf, vf)


def last_kernel(pos_ref, o_ref, l_ref, p_ref, v2_ref, vx_ref, vf_ref, out_ref, wide, sems):
    pos = pos_ref[0]
    set_ones(wide)
    fetch(
        [
            (when, widened(source, wide))
            for when, source in second_choices(pos, vf_ref, vx_ref, v2_ref)
        ],
        sems,
    )
    for h in range(HEADS):
        mine = slice(h * HD, (h + 1) * HD)
        for i in range(ROWS // FAR):
            lo, hi = i * FAR, (i + 1) * FAR
            summed = jnp.dot(
                p_ref[h, lo:hi, :], wide[h // RATIO], preferred_element_type=jnp.float32
            )
            total = l_ref[lo:hi, h : h + 1] + summed[:, HD:]
            out = (o_ref[lo:hi, mine] + summed[:, :HD]) / total
            out_ref[lo:hi, mine] = out.astype(jnp.bfloat16)


def last(pos, o, l, p, v2, vx, vf):
    return pl.pallas_call(
        last_kernel,
        out_shape=jax.ShapeDtypeStruct((ROWS, HEADS * HD), jnp.bfloat16),
        in_specs=[smem()] + [vmem()] * 3 + [anywhere()] * 3,
        out_specs=vmem(),
        scratch_shapes=[block_scratch(), pltpu.SemaphoreType.DMA((2,))],
        compiler_params=pltpu.CompilerParams(vmem_limit_bytes=LIMIT),
        cost_estimate=cost(2 << 30, 5 << 20),
        name="last",
    )(pos, o, l, p, v2, vx, vf)


def shards(queries, keys_next, values_next, keys_front, values_front, keys_prev, values_prev):
    pos = lax.axis_index("seq").astype(jnp.int32).reshape(1)
    k1 = shifted(keys_next)
    v1 = shifted(values_next)
    kx = crossing(keys_next)
    vx = crossing(values_next)
    k2 = inner(k1)
    v2 = inner(v1)
    packed = pack(keys_prev, values_prev)
    arrived = exchange(packed)
    state = main(
        pos, queries, keys_next, values_next, k1, v1, k2, kx,
        keys_front, values_front,
    )
    attended = last(pos, *state, v2, vx, values_front)
    banded_keys, banded_values = unpack(arrived)
    return (attended, banded_keys, banded_values)


def solution(mesh):
    in_specs = (
        P("seq", "head"),
        P("seq", "head"),
        P("seq", "head"),
        P(None, "head"),
        P(None, "head"),
        P("seq", "head"),
        P("seq", "head"),
    )
    out_specs = (P("seq", "head"), P("seq", "head"), P("seq", "head"))
    return jax.shard_map(
        shards, mesh=mesh, in_specs=in_specs, out_specs=out_specs, check_vma=False
    )
```

time: 80.8 us -> 84.8 us (1.050)
  local copies, waits for them, and re-layouts: 1.91 us -> 5.21 us
  starting transfers between devices: 30.5 us -> 33 us
  waiting for transfers between devices: 32.2 us -> 30.8 us
    ppermute x4 -> x2, waiting for transfers between devices: 32.2 us -> 20.5 us  [shifted(): lax.ppermute(value, 'seq', [(source, source + 1) for source in range(coun...]
    ppermute x0 -> x4, waiting for transfers between devices: none -> 10.3 us  [the longest x2 10.3 us: crossing(): return lax.ppermute(value, 'seq', pairs)]
    ppermute x0 -> x4, starting transfers between devices: none -> 6.22 us  [the longest x2 3.64 us: inner(): return lax.ppermute(value, 'seq', pairs)]
    ppermute x4 -> x2, starting transfers between devices: 10.6 us -> 6.76 us  [shifted(): lax.ppermute(value, 'seq', [(source, source + 1) for source in range(coun...]
    unnamed x10, local copies, waits for them, and re-layouts: 1.91 us -> 5.21 us
  transfers between devices with their start and end apart: 5 -> 7, of which waited for: 4 -> 3; matrix products, arithmetic and copies ran while one was open for 0% -> 0% of each run, Pallas kernels for 15% -> 14%
where the time goes in v3:
time: 84.8 us; the launch traced here: 84.3 us
  starting transfers between devices  33 us (39%)
  waiting for transfers between devices  30.8 us (36%)
  Pallas kernels  14.6 us (17%)
  local copies, waits for them, and re-layouts  5.21 us (6%)
    ppermute x2, waiting for transfers between devices, shifted(): lax.ppermute(value, 'seq', [(source, source + 1) for source in range(coun...  20.5 us
    all_to_all x1, starting transfers between devices, exchange(): return lax.all_to_all(x, 'seq', split_axis=0, concat_axis=0, tiled=True)  20 us
    ppermute x2, waiting for transfers between devices, crossing(): return lax.ppermute(value, 'seq', pairs)  10.3 us
    pallas_call x1, Pallas kernels, main(): pl.pallas_call(main_kernel, out_shape=(jax.ShapeDtypeStruct((ROWS, HEADS...  9.07 us
    ppermute x2, starting transfers between devices, shifted(): lax.ppermute(value, 'seq', [(source, source + 1) for source in range(coun...  6.76 us
    unnamed x10, local copies, waits for them, and re-layouts  5.21 us
    ppermute x2, starting transfers between devices, inner(): return lax.ppermute(value, 'seq', pairs)  3.64 us
    ppermute x2, starting transfers between devices, crossing(): return lax.ppermute(value, 'seq', pairs)  2.58 us
  transfers between devices with their start and end apart: 7, of which 3 were waited for; matrix products, arithmetic and copies ran while one was open for 0% of the time, Pallas kernels for 14%

profile of v3, /device:TPU:6, one launch (start us, length us, event | category | flops | bytes accessed | tf_op | source)
XLA Modules:
  0.0 84.3 jit_solution(1995713583973223003)
XLA Ops:
  0.6 2.1 %pack.1 = bf16[1024,256]{1,0:T(8,128)(2,1)} custom-call(bf16[512,256]{1,0:T(8,128)(2,1)} %k_ref.1, bf16[512,256]{1,0:T(8,128)(2,1)} %v_ref.1), custom_call_target="tpu_custom_call" | custom-call | flops 67108864 | bytes 1048576 | tf_op jit(solution)/shard_map/pack/pallas_call | solution.py:75
  2.7 20.0 %all-to-all-start = ((bf16[128,8,256]{2,1,0:T(8,128)(2,1)}), bf16[128,8,256]{2,1,0:T(8,128)(2,1)S(1)}, u32[]{:S(2)}, u32[]{:S(2)}) async-start(bf16[128,8,256]{2,1,0:T(8,128)(2,1)} %bitcast.4), calls=%async_computation | async-start | bytes 1048576 | tf_op jit(solution)/shard_map/all_to_all | solution.py:108
  22.7 3.4 %collective-permute-start = (bf16[512,256]{1,0:T(8,128)(2,1)}, bf16[512,256]{1,0:T(8,128)(2,1)S(1)}, u32[]{:S(2)}, u32[]{:S(2)}) collective-permute-start(bf16[512,256]{1,0:T(8,128)(2,1)} %k0_ref.1), channel_id=1, source_target_pairs={{0,4},{4,8},{8,12},{12,16},{16,20},{20,24},{24,28},{28,32},{32,36}... | collective-permute-start | bytes 786440 | tf_op jit(solution)/shard_map/ppermute | solution.py:25
  26.1 3.4 %collective-permute-start.1 = (bf16[512,256]{1,0:T(8,128)(2,1)}, bf16[512,256]{1,0:T(8,128)(2,1)S(1)}, u32[]{:S(2)}, u32[]{:S(2)}) collective-permute-start(bf16[512,256]{1,0:T(8,128)(2,1)} %v0_ref.1), channel_id=1, source_target_pairs={{0,4},{4,8},{8,12},{12,16},{16,20},{20,24},{24,28},{28,32},{32,36}... | collective-permute-start | bytes 786440 | tf_op jit(solution)/shard_map/ppermute | solution.py:25
  29.5 1.3 %collective-permute-start.3 = (bf16[512,256]{1,0:T(8,128)(2,1)}, bf16[512,256]{1,0:T(8,128)(2,1)S(1)}, u32[]{:S(2)}, u32[]{:S(2)}) collective-permute-start(bf16[512,256]{1,0:T(8,128)(2,1)} %k0_ref.1), channel_id=1, source_target_pairs={{24,32},{56,64},{88,96},{120,128},{152,160},{184,192},{216,224},{2... | collective-permute-start | bytes 786440 | tf_op jit(solution)/shard_map/ppermute | solution.py:31
  30.8 18.9 %collective-permute-done.k1_ref = bf16[512,256]{1,0:T(8,128)(2,1)S(1)} collective-permute-done((bf16[512,256]{1,0:T(8,128)(2,1)}, bf16[512,256]{1,0:T(8,128)(2,1)S(1)}, u32[]{:S(2)}, u32[]{:S(2)}) %collective-permute-start) | collective-permute-done | bytes 262176 | tf_op jit(solution)/shard_map/ppermute | solution.py:25
  49.6 1.3 %collective-permute-start.2 = (bf16[512,256]{1,0:T(8,128)(2,1)S(1)}, bf16[512,256]{1,0:T(8,128)(2,1)S(1)}, u32[]{:S(2)}, u32[]{:S(2)}) collective-permute-start(bf16[512,256]{1,0:T(8,128)(2,1)S(1)} %collective-permute-done.k1_ref), channel_id=1, source_target_pairs={{0,4},{4,8},{8,12},{12,16},{16,20},{20,24},{24,28},{32,36},{36,40}... | collective-permute-start | bytes 786440 | tf_op jit(solution)/shard_map/ppermute | solution.py:37
  51.0 1.3 %collective-permute-start.5 = (bf16[512,256]{1,0:T(8,128)(2,1)}, bf16[512,256]{1,0:T(8,128)(2,1)S(1)}, u32[]{:S(2)}, u32[]{:S(2)}) collective-permute-start(bf16[512,256]{1,0:T(8,128)(2,1)} %v0_ref.1), channel_id=1, source_target_pairs={{24,32},{56,64},{88,96},{120,128},{152,160},{184,192},{216,224},{2... | collective-permute-start | bytes 786440 | tf_op jit(solution)/shard_map/ppermute | solution.py:31
  52.3 1.6 %collective-permute-done.1.v1_ref = bf16[512,256]{1,0:T(8,128)(2,1)S(1)} collective-permute-done((bf16[512,256]{1,0:T(8,128)(2,1)}, bf16[512,256]{1,0:T(8,128)(2,1)S(1)}, u32[]{:S(2)}, u32[]{:S(2)}) %collective-permute-start.1) | collective-permute-done | bytes 262176 | tf_op jit(solution)/shard_map/ppermute | solution.py:25
  53.9 2.3 %collective-permute-start.4 = (bf16[512,256]{1,0:T(8,128)(2,1)S(1)}, bf16[512,256]{1,0:T(8,128)(2,1)S(1)}, u32[]{:S(2)}, u32[]{:S(2)}) collective-permute-start(bf16[512,256]{1,0:T(8,128)(2,1)S(1)} %collective-permute-done.1.v1_ref), channel_id=1, source_target_pairs={{0,4},{4,8},{8,12},{12,16},{16,20},{20,24},{24,28},{32,36},{36,40}... | collective-permute-start | bytes 786440 | tf_op jit(solution)/shard_map/ppermute | solution.py:37
  56.2 10.3 %collective-permute-done.3.kx_ref = bf16[512,256]{1,0:T(8,128)(2,1)S(1)} collective-permute-done((bf16[512,256]{1,0:T(8,128)(2,1)}, bf16[512,256]{1,0:T(8,128)(2,1)S(1)}, u32[]{:S(2)}, u32[]{:S(2)}) %collective-permute-start.3) | collective-permute-done | bytes 262176 | tf_op jit(solution)/shard_map/ppermute | solution.py:31
  66.5 0.0 collective-permute-done.2.k2_ref
  66.5 0.0 copy-start
  66.5 1.0 %copy-done = bf16[1024,256]{1,0:T(8,128)(2,1)S(1)} copy-done((bf16[1024,256]{1,0:T(8,128)(2,1)S(1)}, bf16[1024,256]{1,0:T(8,128)(2,1)}, u32[]{:S(2)}) %copy-start) | copy-done | bytes 524312
  67.6 1.2 %copy-done.1 = bf16[512,1024]{1,0:T(8,128)(2,1)S(1)} copy-done((bf16[512,1024]{1,0:T(8,128)(2,1)S(1)}, bf16[512,1024]{1,0:T(8,128)(2,1)}, u32[]{:S(2)}) %copy-start.1) | copy-done | bytes 1048600
  68.8 1.0 %copy-done.2 = bf16[1024,256]{1,0:T(8,128)(2,1)S(1)} copy-done((bf16[1024,256]{1,0:T(8,128)(2,1)S(1)}, bf16[1024,256]{1,0:T(8,128)(2,1)}, u32[]{:S(2)}) %copy-start.2) | copy-done | bytes 524312
  69.8 0.9 %copy-done.3 = bf16[512,256]{1,0:T(8,128)(2,1)S(1)} copy-done((bf16[512,256]{1,0:T(8,128)(2,1)S(1)}, bf16[512,256]{1,0:T(8,128)(2,1)}, u32[]{:S(2)}) %copy-start.3) | copy-done | bytes 262168
  70.8 0.9 %copy-done.4 = bf16[512,256]{1,0:T(8,128)(2,1)S(1)} copy-done((bf16[512,256]{1,0:T(8,128)(2,1)S(1)}, bf16[512,256]{1,0:T(8,128)(2,1)}, u32[]{:S(2)}) %copy-start.4) | copy-done | bytes 262168
  71.7 9.1 %main.1 = (f32[512,1024]{1,0:T(8,128)S(1)}, f32[512,128]{1,0:T(8,128)S(1)}, bf16[8,512,512]{2,1,0:T(8,128)(2,1)S(1)}) custom-call(s32[1]{0:T(128)} %bitcast.pos_ref, bf16[512,1024]{1,0:T(8,128)(2,1)S(1)} %copy-done.1, bf16[512,256]{1,0:T(8,128)(2,1)S(1)} %copy-done.3, bf16[512,256]{1,0:T(8,128)(2,1)S(1)} %copy-done.4, ...), custom_call_target="tpu_custom_call" | custom-call | flops 5368709120 | bytes 10485760 | tf_op jit(solution)/shard_map/main/pallas_call | solution.py:212
  80.8 0.0 collective-permute-done.5.vx_ref
  80.8 0.0 collective-permute-done.4.v2_ref
  80.8 2.4 %last.1 = bf16[512,1024]{1,0:T(8,128)(2,1)} custom-call(s32[1]{0:T(128)} %bitcast.pos_ref, f32[512,1024]{1,0:T(8,128)S(1)} %get-tuple-element.8.o_ref, f32[512,128]{1,0:T(8,128)S(1)} %get-tuple-element.9.l_ref, bf16[8,512,512]{2,1,0:T(8,128)(2,1)S(1)} %get-tuple-element.10.p_ref, bf16[512,256]{1,0:T(8,128)(2,1)S(1)} %collective-permute-done.4.v2_ref, ...), custom_call_target="tpu_custom_call" | custom-call | flops 2147483648 | bytes 5242880 | tf_op jit(solution)/shard_map/last/pallas_call | solution.py:257
  83.2 0.0 all-to-all-done
  83.2 1.1 %unpack.1 = (bf16[512,256]{1,0:T(8,128)(2,1)}, bf16[512,256]{1,0:T(8,128)(2,1)}) custom-call(bf16[1024,256]{1,0:T(8,128)(2,1)S(1)} %bitcast.3), custom_call_target="tpu_custom_call" | custom-call | flops 67108864 | bytes 1048576 | tf_op jit(solution)/shard_map/unpack/pallas_call | solution.py:96
  (4 shorter events, 0.0 us)
Async XLA Ops:
  2.7 80.5 %all-to-all-start = ((bf16[128,8,256]{2,1,0:T(8,128)(2,1)}), bf16[128,8,256]{2,1,0:T(8,128)(2,1)S(1)}, u32[]{:S(2)}, u32[]{:S(2)}) async-start(bf16[128,8,256]{2,1,0:T(8,128)(2,1)} %bitcast.4), calls=%async_computation | async-start | bytes 1048576 | tf_op jit(solution)/shard_map/all_to_all | solution.py:108
  22.7 26.9 %collective-permute-start = (bf16[512,256]{1,0:T(8,128)(2,1)}, bf16[512,256]{1,0:T(8,128)(2,1)S(1)}, u32[]{:S(2)}, u32[]{:S(2)}) collective-permute-start(bf16[512,256]{1,0:T(8,128)(2,1)} %k0_ref.1), channel_id=1, source_target_pairs={{0,4},{4,8},{8,12},{12,16},{16,20},{20,24},{24,28},{28,32},{32,36}... | collective-permute-start | bytes 786440 | tf_op jit(solution)/shard_map/ppermute | solution.py:25
  26.1 27.7 %collective-permute-start.1 = (bf16[512,256]{1,0:T(8,128)(2,1)}, bf16[512,256]{1,0:T(8,128)(2,1)S(1)}, u32[]{:S(2)}, u32[]{:S(2)}) collective-permute-start(bf16[512,256]{1,0:T(8,128)(2,1)} %v0_ref.1), channel_id=1, source_target_pairs={{0,4},{4,8},{8,12},{12,16},{16,20},{20,24},{24,28},{28,32},{32,36}... | collective-permute-start | bytes 786440 | tf_op jit(solution)/shard_map/ppermute | solution.py:25
  29.5 37.0 %collective-permute-start.3 = (bf16[512,256]{1,0:T(8,128)(2,1)}, bf16[512,256]{1,0:T(8,128)(2,1)S(1)}, u32[]{:S(2)}, u32[]{:S(2)}) collective-permute-start(bf16[512,256]{1,0:T(8,128)(2,1)} %k0_ref.1), channel_id=1, source_target_pairs={{24,32},{56,64},{88,96},{120,128},{152,160},{184,192},{216,224},{2... | collective-permute-start | bytes 786440 | tf_op jit(solution)/shard_map/ppermute | solution.py:31
  49.6 16.9 %collective-permute-start.2 = (bf16[512,256]{1,0:T(8,128)(2,1)S(1)}, bf16[512,256]{1,0:T(8,128)(2,1)S(1)}, u32[]{:S(2)}, u32[]{:S(2)}) collective-permute-start(bf16[512,256]{1,0:T(8,128)(2,1)S(1)} %collective-permute-done.k1_ref), channel_id=1, source_target_pairs={{0,4},{4,8},{8,12},{12,16},{16,20},{20,24},{24,28},{32,36},{36,40}... | collective-permute-start | bytes 786440 | tf_op jit(solution)/shard_map/ppermute | solution.py:37
  51.0 29.9 %collective-permute-start.5 = (bf16[512,256]{1,0:T(8,128)(2,1)}, bf16[512,256]{1,0:T(8,128)(2,1)S(1)}, u32[]{:S(2)}, u32[]{:S(2)}) collective-permute-start(bf16[512,256]{1,0:T(8,128)(2,1)} %v0_ref.1), channel_id=1, source_target_pairs={{24,32},{56,64},{88,96},{120,128},{152,160},{184,192},{216,224},{2... | collective-permute-start | bytes 786440 | tf_op jit(solution)/shard_map/ppermute | solution.py:31
  53.9 27.0 %collective-permute-start.4 = (bf16[512,256]{1,0:T(8,128)(2,1)S(1)}, bf16[512,256]{1,0:T(8,128)(2,1)S(1)}, u32[]{:S(2)}, u32[]{:S(2)}) collective-permute-start(bf16[512,256]{1,0:T(8,128)(2,1)S(1)} %collective-permute-done.1.v1_ref), channel_id=1, source_target_pairs={{0,4},{4,8},{8,12},{12,16},{16,20},{20,24},{24,28},{32,36},{36,40}... | collective-permute-start | bytes 786440 | tf_op jit(solution)/shard_map/ppermute | solution.py:37
  66.5 1.0 %copy-start = (bf16[1024,256]{1,0:T(8,128)(2,1)S(1)}, bf16[1024,256]{1,0:T(8,128)(2,1)}, u32[]{:S(2)}) copy-start(bf16[1024,256]{1,0:T(8,128)(2,1)} %vf_ref.3) | copy-start | bytes 1572868
  67.6 1.2 %copy-start.1 = (bf16[512,1024]{1,0:T(8,128)(2,1)S(1)}, bf16[512,1024]{1,0:T(8,128)(2,1)}, u32[]{:S(2)}) copy-start(bf16[512,1024]{1,0:T(8,128)(2,1)} %q_ref.1) | copy-start | bytes 3145732
  68.8 1.0 %copy-start.2 = (bf16[1024,256]{1,0:T(8,128)(2,1)S(1)}, bf16[1024,256]{1,0:T(8,128)(2,1)}, u32[]{:S(2)}) copy-start(bf16[1024,256]{1,0:T(8,128)(2,1)} %kf_ref.1) | copy-start | bytes 1572868
  69.8 0.9 %copy-start.3 = (bf16[512,256]{1,0:T(8,128)(2,1)S(1)}, bf16[512,256]{1,0:T(8,128)(2,1)}, u32[]{:S(2)}) copy-start(bf16[512,256]{1,0:T(8,128)(2,1)} %k0_ref.1) | copy-start | bytes 786436
  70.8 0.9 %copy-start.4 = (bf16[512,256]{1,0:T(8,128)(2,1)S(1)}, bf16[512,256]{1,0:T(8,128)(2,1)}, u32[]{:S(2)}) copy-start(bf16[512,256]{1,0:T(8,128)(2,1)} %v0_ref.1) | copy-start | bytes 786436

commit v4 on v3

--- a/solution.py
+++ b/solution.py
@@ -83,12 +83,21 @@
     return packed.reshape(ROWS // 4, 8, WIDTH)
 
 
-def unpack_kernel(x_ref, k_ref, v_ref):
+def unpack_kernel(x_ref, k_ref, v_ref, k_buf, v_buf, sems):
     pick = chooser(128, lambda r: ((r >> 2) & 15) * 8 + (r >> 6) * 4 + (r & 3))
+    copies = []
     for c in range(8):
         moved = moved_by(pick, [x_ref[pl.ds(c * 128, 128), :]])
-        k_ref[pl.ds(c * 64, 64), :] = moved[:64]
-        v_ref[pl.ds(c * 64, 64), :] = moved[64:]
+        k_buf[pl.ds(c * 64, 64), :] = moved[:64]
+        v_buf[pl.ds(c * 64, 64), :] = moved[64:]
+        if c % 2 == 1:
+            span = pl.ds((c - 1) * 64, 128)
+            for n, (buf, ref) in enumerate(((k_buf, k_ref), (v_buf, v_ref))):
+                copy = pltpu.make_async_copy(buf.at[span], ref.at[span], sems.at[n, c // 2])
+                copy.start()
+                copies.append(copy)
+    for copy in copies:
+        copy.wait()
 
 
 def unpack(x):
@@ -97,7 +106,12 @@
         unpack_kernel,
         out_shape=(shape, shape),
         in_specs=[vmem()],
-        out_specs=(vmem(), vmem()),
+        out_specs=(anywhere(), anywhere()),
+        scratch_shapes=[
+            pltpu.VMEM((ROWS, WIDTH), jnp.bfloat16),
+            pltpu.VMEM((ROWS, WIDTH), jnp.bfloat16),
+            pltpu.SemaphoreType.DMA((2, 4)),
+        ],
         compiler_params=pltpu.CompilerParams(vmem_limit_bytes=8 << 20),
         cost_estimate=cost(1 << 26, 1 << 20),
         name="unpack",
@@ -231,7 +245,9 @@
     )(pos, q, k0, v0, k1, v1, k2, kx, kf, vf)
 
 
-def last_kernel(pos_ref, o_ref, l_ref, p_ref, v2_ref, vx_ref, vf_ref, out_ref, wide, sems):
+def last_kernel(
+    pos_ref, o_ref, l_ref, p_ref, v2_ref, vx_ref, vf_ref, out_ref, wide, out_buf, sems, out_sems
+):
     pos = pos_ref[0]
     set_ones(wide)
     fetch(
@@ -241,6 +257,7 @@
         ],
         sems,
     )
+    copies = []
     for h in range(HEADS):
         mine = slice(h * HD, (h + 1) * HD)
         for i in range(ROWS // FAR):
@@ -250,7 +267,16 @@
             )
             total = l_ref[lo:hi, h : h + 1] + summed[:, HD:]
             out = (o_ref[lo:hi, mine] + summed[:, :HD]) / total
-            out_ref[lo:hi, mine] = out.astype(jnp.bfloat16)
+            out_buf[lo:hi, mine] = out.astype(jnp.bfloat16)
+        if h % 2 == 1:
+            pair = pl.ds((h - 1) * HD, 2 * HD)
+            copy = pltpu.make_async_copy(
+                out_buf.at[:, pair], out_ref.at[:, pair], out_sems.at[h // 2]
+            )
+            copy.start()
+            copies.append(copy)
+    for copy in copies:
+        copy.wait()
 
 
 def last(pos, o, l, p, v2, vx, vf):
@@ -258,8 +284,13 @@
         last_kernel,
         out_shape=jax.ShapeDtypeStruct((ROWS, HEADS * HD), jnp.bfloat16),
         in_specs=[smem()] + [vmem()] * 3 + [anywhere()] * 3,
-        out_specs=vmem(),
-        scratch_shapes=[block_scratch(), pltpu.SemaphoreType.DMA((2,))],
+        out_specs=anywhere(),
+        scratch_shapes=[
+            block_scratch(),
+            pltpu.VMEM((ROWS, HEADS * HD), jnp.bfloat16),
+            pltpu.SemaphoreType.DMA((2,)),
+            pltpu.SemaphoreType.DMA((HEADS // 2,)),
+        ],
         compiler_params=pltpu.CompilerParams(vmem_limit_bytes=LIMIT),
         cost_estimate=cost(2 << 30, 5 << 20),
         name="last",

time: 84.8 us -> 84.5 us (level)
  transfers between devices with their start and end apart: 7 -> 7, of which waited for: 3 -> 3; matrix products, arithmetic and copies ran while one was open for 0% -> 0% of each run, Pallas kernels for 14% -> 13%
where the time goes in v4:
time: 84.5 us; the launch traced here: 84 us
  starting transfers between devices  33 us (39%)
  waiting for transfers between devices  30.8 us (36%)
  Pallas kernels  14.3 us (17%)
  local copies, waits for them, and re-layouts  5.21 us (6%)
    ppermute x2, waiting for transfers between devices, shifted(): lax.ppermute(value, 'seq', [(source, source + 1) for source in range(coun...  20.5 us
    all_to_all x1, starting transfers between devices, exchange(): return lax.all_to_all(x, 'seq', split_axis=0, concat_axis=0, tiled=True)  20 us
    ppermute x2, waiting for transfers between devices, crossing(): return lax.ppermute(value, 'seq', pairs)  10.3 us
    pallas_call x1, Pallas kernels, main(): pl.pallas_call(main_kernel, out_shape=(jax.ShapeDtypeStruct((ROWS, HEADS...  9.07 us
    ppermute x2, starting transfers between devices, shifted(): lax.ppermute(value, 'seq', [(source, source + 1) for source in range(coun...  6.76 us
    unnamed x10, local copies, waits for them, and re-layouts  5.21 us
    ppermute x2, starting transfers between devices, inner(): return lax.ppermute(value, 'seq', pairs)  3.64 us
    ppermute x2, starting transfers between devices, crossing(): return lax.ppermute(value, 'seq', pairs)  2.58 us
  transfers between devices with their start and end apart: 7, of which 3 were waited for; matrix products, arithmetic and copies ran while one was open for 0% of the time, Pallas kernels for 13%

profile of v4, /device:TPU:6, one launch (start us, length us, event | category | flops | bytes accessed | tf_op | source)
XLA Modules:
  0.0 84.0 jit_solution(13663526935492862885)
XLA Ops:
  0.6 2.1 %pack.1 = bf16[1024,256]{1,0:T(8,128)(2,1)} custom-call(bf16[512,256]{1,0:T(8,128)(2,1)} %k_ref.1, bf16[512,256]{1,0:T(8,128)(2,1)} %v_ref.1), custom_call_target="tpu_custom_call" | custom-call | flops 67108864 | bytes 1048576 | tf_op jit(solution)/shard_map/pack/pallas_call | solution.py:75
  2.7 20.0 %all-to-all-start = ((bf16[128,8,256]{2,1,0:T(8,128)(2,1)}), bf16[128,8,256]{2,1,0:T(8,128)(2,1)S(1)}, u32[]{:S(2)}, u32[]{:S(2)}) async-start(bf16[128,8,256]{2,1,0:T(8,128)(2,1)} %bitcast.4), calls=%async_computation | async-start | bytes 1048576 | tf_op jit(solution)/shard_map/all_to_all | solution.py:122
  22.7 3.4 %collective-permute-start = (bf16[512,256]{1,0:T(8,128)(2,1)}, bf16[512,256]{1,0:T(8,128)(2,1)S(1)}, u32[]{:S(2)}, u32[]{:S(2)}) collective-permute-start(bf16[512,256]{1,0:T(8,128)(2,1)} %k0_ref.1), channel_id=1, source_target_pairs={{0,4},{4,8},{8,12},{12,16},{16,20},{20,24},{24,28},{28,32},{32,36}... | collective-permute-start | bytes 786440 | tf_op jit(solution)/shard_map/ppermute | solution.py:25
  26.1 3.4 %collective-permute-start.1 = (bf16[512,256]{1,0:T(8,128)(2,1)}, bf16[512,256]{1,0:T(8,128)(2,1)S(1)}, u32[]{:S(2)}, u32[]{:S(2)}) collective-permute-start(bf16[512,256]{1,0:T(8,128)(2,1)} %v0_ref.1), channel_id=1, source_target_pairs={{0,4},{4,8},{8,12},{12,16},{16,20},{20,24},{24,28},{28,32},{32,36}... | collective-permute-start | bytes 786440 | tf_op jit(solution)/shard_map/ppermute | solution.py:25
  29.5 1.3 %collective-permute-start.3 = (bf16[512,256]{1,0:T(8,128)(2,1)}, bf16[512,256]{1,0:T(8,128)(2,1)S(1)}, u32[]{:S(2)}, u32[]{:S(2)}) collective-permute-start(bf16[512,256]{1,0:T(8,128)(2,1)} %k0_ref.1), channel_id=1, source_target_pairs={{24,32},{56,64},{88,96},{120,128},{152,160},{184,192},{216,224},{2... | collective-permute-start | bytes 786440 | tf_op jit(solution)/shard_map/ppermute | solution.py:31
  30.8 18.9 %collective-permute-done.k1_ref = bf16[512,256]{1,0:T(8,128)(2,1)S(1)} collective-permute-done((bf16[512,256]{1,0:T(8,128)(2,1)}, bf16[512,256]{1,0:T(8,128)(2,1)S(1)}, u32[]{:S(2)}, u32[]{:S(2)}) %collective-permute-start) | collective-permute-done | bytes 262176 | tf_op jit(solution)/shard_map/ppermute | solution.py:25
  49.6 1.3 %collective-permute-start.2 = (bf16[512,256]{1,0:T(8,128)(2,1)S(1)}, bf16[512,256]{1,0:T(8,128)(2,1)S(1)}, u32[]{:S(2)}, u32[]{:S(2)}) collective-permute-start(bf16[512,256]{1,0:T(8,128)(2,1)S(1)} %collective-permute-done.k1_ref), channel_id=1, source_target_pairs={{0,4},{4,8},{8,12},{12,16},{16,20},{20,24},{24,28},{32,36},{36,40}... | collective-permute-start | bytes 786440 | tf_op jit(solution)/shard_map/ppermute | solution.py:37
  51.0 1.3 %collective-permute-start.5 = (bf16[512,256]{1,0:T(8,128)(2,1)}, bf16[512,256]{1,0:T(8,128)(2,1)S(1)}, u32[]{:S(2)}, u32[]{:S(2)}) collective-permute-start(bf16[512,256]{1,0:T(8,128)(2,1)} %v0_ref.1), channel_id=1, source_target_pairs={{24,32},{56,64},{88,96},{120,128},{152,160},{184,192},{216,224},{2... | collective-permute-start | bytes 786440 | tf_op jit(solution)/shard_map/ppermute | solution.py:31
  52.3 1.6 %collective-permute-done.1.v1_ref = bf16[512,256]{1,0:T(8,128)(2,1)S(1)} collective-permute-done((bf16[512,256]{1,0:T(8,128)(2,1)}, bf16[512,256]{1,0:T(8,128)(2,1)S(1)}, u32[]{:S(2)}, u32[]{:S(2)}) %collective-permute-start.1) | collective-permute-done | bytes 262176 | tf_op jit(solution)/shard_map/ppermute | solution.py:25
  53.9 2.3 %collective-permute-start.4 = (bf16[512,256]{1,0:T(8,128)(2,1)S(1)}, bf16[512,256]{1,0:T(8,128)(2,1)S(1)}, u32[]{:S(2)}, u32[]{:S(2)}) collective-permute-start(bf16[512,256]{1,0:T(8,128)(2,1)S(1)} %collective-permute-done.1.v1_ref), channel_id=1, source_target_pairs={{0,4},{4,8},{8,12},{12,16},{16,20},{20,24},{24,28},{32,36},{36,40}... | collective-permute-start | bytes 786440 | tf_op jit(solution)/shard_map/ppermute | solution.py:37
  56.2 10.3 %collective-permute-done.3.kx_ref = bf16[512,256]{1,0:T(8,128)(2,1)S(1)} collective-permute-done((bf16[512,256]{1,0:T(8,128)(2,1)}, bf16[512,256]{1,0:T(8,128)(2,1)S(1)}, u32[]{:S(2)}, u32[]{:S(2)}) %collective-permute-start.3) | collective-permute-done | bytes 262176 | tf_op jit(solution)/shard_map/ppermute | solution.py:31
  66.5 0.0 collective-permute-done.2.k2_ref
  66.5 0.0 copy-start
  66.5 1.0 %copy-done = bf16[1024,256]{1,0:T(8,128)(2,1)S(1)} copy-done((bf16[1024,256]{1,0:T(8,128)(2,1)S(1)}, bf16[1024,256]{1,0:T(8,128)(2,1)}, u32[]{:S(2)}) %copy-start) | copy-done | bytes 524312
  67.6 1.2 %copy-done.1 = bf16[512,1024]{1,0:T(8,128)(2,1)S(1)} copy-done((bf16[512,1024]{1,0:T(8,128)(2,1)S(1)}, bf16[512,1024]{1,0:T(8,128)(2,1)}, u32[]{:S(2)}) %copy-start.1) | copy-done | bytes 1048600
  68.8 1.0 %copy-done.2 = bf16[1024,256]{1,0:T(8,128)(2,1)S(1)} copy-done((bf16[1024,256]{1,0:T(8,128)(2,1)S(1)}, bf16[1024,256]{1,0:T(8,128)(2,1)}, u32[]{:S(2)}) %copy-start.2) | copy-done | bytes 524312
  69.8 0.9 %copy-done.3 = bf16[512,256]{1,0:T(8,128)(2,1)S(1)} copy-done((bf16[512,256]{1,0:T(8,128)(2,1)S(1)}, bf16[512,256]{1,0:T(8,128)(2,1)}, u32[]{:S(2)}) %copy-start.3) | copy-done | bytes 262168
  70.8 0.9 %copy-done.4 = bf16[512,256]{1,0:T(8,128)(2,1)S(1)} copy-done((bf16[512,256]{1,0:T(8,128)(2,1)S(1)}, bf16[512,256]{1,0:T(8,128)(2,1)}, u32[]{:S(2)}) %copy-start.4) | copy-done | bytes 262168
  71.7 9.1 %main.1 = (f32[512,1024]{1,0:T(8,128)S(1)}, f32[512,128]{1,0:T(8,128)S(1)}, bf16[8,512,512]{2,1,0:T(8,128)(2,1)S(1)}) custom-call(s32[1]{0:T(128)} %bitcast.pos_ref, bf16[512,1024]{1,0:T(8,128)(2,1)S(1)} %copy-done.1, bf16[512,256]{1,0:T(8,128)(2,1)S(1)} %copy-done.3, bf16[512,256]{1,0:T(8,128)(2,1)S(1)} %copy-done.4, ...), custom_call_target="tpu_custom_call" | custom-call | flops 5368709120 | bytes 10485760 | tf_op jit(solution)/shard_map/main/pallas_call | solution.py:226
  80.8 0.0 collective-permute-done.5.vx_ref
  80.8 0.0 collective-permute-done.4.v2_ref
  80.8 2.1 %last.1 = bf16[512,1024]{1,0:T(8,128)(2,1)} custom-call(s32[1]{0:T(128)} %bitcast.pos_ref, f32[512,1024]{1,0:T(8,128)S(1)} %get-tuple-element.8.o_ref, f32[512,128]{1,0:T(8,128)S(1)} %get-tuple-element.9.l_ref, bf16[8,512,512]{2,1,0:T(8,128)(2,1)S(1)} %get-tuple-element.10.p_ref, bf16[512,256]{1,0:T(8,128)(2,1)S(1)} %collective-permute-done.4.v2_ref, ...), custom_call_target="tpu_custom_call" | custom-call | flops 2147483648 | bytes 5242880 | tf_op jit(solution)/shard_map/last/pallas_call | solution.py:283
  83.0 0.0 all-to-all-done
  83.0 1.0 %unpack.1 = (bf16[512,256]{1,0:T(8,128)(2,1)}, bf16[512,256]{1,0:T(8,128)(2,1)}) custom-call(bf16[1024,256]{1,0:T(8,128)(2,1)S(1)} %bitcast.3), custom_call_target="tpu_custom_call" | custom-call | flops 67108864 | bytes 1048576 | tf_op jit(solution)/shard_map/unpack/pallas_call | solution.py:105
  (4 shorter events, 0.0 us)
Async XLA Ops:
  2.7 80.2 %all-to-all-start = ((bf16[128,8,256]{2,1,0:T(8,128)(2,1)}), bf16[128,8,256]{2,1,0:T(8,128)(2,1)S(1)}, u32[]{:S(2)}, u32[]{:S(2)}) async-start(bf16[128,8,256]{2,1,0:T(8,128)(2,1)} %bitcast.4), calls=%async_computation | async-start | bytes 1048576 | tf_op jit(solution)/shard_map/all_to_all | solution.py:122
  22.7 26.9 %collective-permute-start = (bf16[512,256]{1,0:T(8,128)(2,1)}, bf16[512,256]{1,0:T(8,128)(2,1)S(1)}, u32[]{:S(2)}, u32[]{:S(2)}) collective-permute-start(bf16[512,256]{1,0:T(8,128)(2,1)} %k0_ref.1), channel_id=1, source_target_pairs={{0,4},{4,8},{8,12},{12,16},{16,20},{20,24},{24,28},{28,32},{32,36}... | collective-permute-start | bytes 786440 | tf_op jit(solution)/shard_map/ppermute | solution.py:25
  26.1 27.7 %collective-permute-start.1 = (bf16[512,256]{1,0:T(8,128)(2,1)}, bf16[512,256]{1,0:T(8,128)(2,1)S(1)}, u32[]{:S(2)}, u32[]{:S(2)}) collective-permute-start(bf16[512,256]{1,0:T(8,128)(2,1)} %v0_ref.1), channel_id=1, source_target_pairs={{0,4},{4,8},{8,12},{12,16},{16,20},{20,24},{24,28},{28,32},{32,36}... | collective-permute-start | bytes 786440 | tf_op jit(solution)/shard_map/ppermute | solution.py:25
  29.5 37.0 %collective-permute-start.3 = (bf16[512,256]{1,0:T(8,128)(2,1)}, bf16[512,256]{1,0:T(8,128)(2,1)S(1)}, u32[]{:S(2)}, u32[]{:S(2)}) collective-permute-start(bf16[512,256]{1,0:T(8,128)(2,1)} %k0_ref.1), channel_id=1, source_target_pairs={{24,32},{56,64},{88,96},{120,128},{152,160},{184,192},{216,224},{2... | collective-permute-start | bytes 786440 | tf_op jit(solution)/shard_map/ppermute | solution.py:31
  49.6 16.9 %collective-permute-start.2 = (bf16[512,256]{1,0:T(8,128)(2,1)S(1)}, bf16[512,256]{1,0:T(8,128)(2,1)S(1)}, u32[]{:S(2)}, u32[]{:S(2)}) collective-permute-start(bf16[512,256]{1,0:T(8,128)(2,1)S(1)} %collective-permute-done.k1_ref), channel_id=1, source_target_pairs={{0,4},{4,8},{8,12},{12,16},{16,20},{20,24},{24,28},{32,36},{36,40}... | collective-permute-start | bytes 786440 | tf_op jit(solution)/shard_map/ppermute | solution.py:37
  51.0 29.9 %collective-permute-start.5 = (bf16[512,256]{1,0:T(8,128)(2,1)}, bf16[512,256]{1,0:T(8,128)(2,1)S(1)}, u32[]{:S(2)}, u32[]{:S(2)}) collective-permute-start(bf16[512,256]{1,0:T(8,128)(2,1)} %v0_ref.1), channel_id=1, source_target_pairs={{24,32},{56,64},{88,96},{120,128},{152,160},{184,192},{216,224},{2... | collective-permute-start | bytes 786440 | tf_op jit(solution)/shard_map/ppermute | solution.py:31
  53.9 27.0 %collective-permute-start.4 = (bf16[512,256]{1,0:T(8,128)(2,1)S(1)}, bf16[512,256]{1,0:T(8,128)(2,1)S(1)}, u32[]{:S(2)}, u32[]{:S(2)}) collective-permute-start(bf16[512,256]{1,0:T(8,128)(2,1)S(1)} %collective-permute-done.1.v1_ref), channel_id=1, source_target_pairs={{0,4},{4,8},{8,12},{12,16},{16,20},{20,24},{24,28},{32,36},{36,40}... | collective-permute-start | bytes 786440 | tf_op jit(solution)/shard_map/ppermute | solution.py:37
  66.5 1.0 %copy-start = (bf16[1024,256]{1,0:T(8,128)(2,1)S(1)}, bf16[1024,256]{1,0:T(8,128)(2,1)}, u32[]{:S(2)}) copy-start(bf16[1024,256]{1,0:T(8,128)(2,1)} %vf_ref.3) | copy-start | bytes 1572868
  67.6 1.2 %copy-start.1 = (bf16[512,1024]{1,0:T(8,128)(2,1)S(1)}, bf16[512,1024]{1,0:T(8,128)(2,1)}, u32[]{:S(2)}) copy-start(bf16[512,1024]{1,0:T(8,128)(2,1)} %q_ref.1) | copy-start | bytes 3145732
  68.8 1.0 %copy-start.2 = (bf16[1024,256]{1,0:T(8,128)(2,1)S(1)}, bf16[1024,256]{1,0:T(8,128)(2,1)}, u32[]{:S(2)}) copy-start(bf16[1024,256]{1,0:T(8,128)(2,1)} %kf_ref.1) | copy-start | bytes 1572868
  69.8 0.9 %copy-start.3 = (bf16[512,256]{1,0:T(8,128)(2,1)S(1)}, bf16[512,256]{1,0:T(8,128)(2,1)}, u32[]{:S(2)}) copy-start(bf16[512,256]{1,0:T(8,128)(2,1)} %k0_ref.1) | copy-start | bytes 786436
  70.8 0.9 %copy-start.4 = (bf16[512,256]{1,0:T(8,128)(2,1)S(1)}, bf16[512,256]{1,0:T(8,128)(2,1)}, u32[]{:S(2)}) copy-start(bf16[512,256]{1,0:T(8,128)(2,1)} %v0_ref.1) | copy-start | bytes 786436
